TPU v7x, 768 devices: a whole 4x8x12 slice. The times are simulated.
768 devices in a mesh: dom: 32 (over z_lo, x, core), wf: 24 (over y, z_hi).
Axes of the slice: x: 4, y: 8, z: 12 (z_hi: 3, z_lo: 4; z = z_hi * 4 + z_lo), core: 2. Of those that a mesh axis runs over, the one named last changes fastest.
Arguments:
- wavefunctions: float32 [16384, 3072], P('dom', 'wf'), may hold values from -80 to 80
- cell_matrix: bfloat16 [64, 512, 512], P('dom'), may hold values from -1 to 4, as said below
- cell_nodes: int32 [64, 512], P('dom'), may hold values from 0 to 767, as said below
- home_counts: int32 [32, 3], P('dom'), may hold values from 0 to 4, as said below
- atom_start: int32 [32, 3, 4], P('dom'), may hold values from 0 to 256
- projectors: bfloat16 [32, 3, 4, 18, 256], P('dom'), may hold values from -0.375 to 0.375
- coupling: float32 [128, 18, 18], P('dom'), may hold values from -3 to 3
Outputs:
- filtered: float32 [16384, 3072], P('dom', 'wf')
- block_norm: float32 [], replicated
Inputs may be any that keep to these rules, and one draw needn't show every extreme that they name: `cell_nodes`: each cell lists 512 distinct rows of its domain's extended numbering. home_counts[d, k] depends only on the home domain d - 1 + k and is the same on every domain that lists it; it is 0 for homes outside the grid and 1 to 4 otherwise. `cell_matrix`: each matrix is symmetric.
All inputs are finite; a program needn't handle non-finite values.
Results may differ from a plain program's by a relative error of at most 0.0056.
Values may be sent and summed in bfloat16 or wider, within the bound.
A program may use at most 32 MiB of HBM per device.

v0:
```python
import jax
import jax.numpy as jnp
from jax import lax
from jax.sharding import PartitionSpec as P

lower_edge = -1.0
cut_edge = 2.0
upper_edge = 9.0


def with_halo(array, sides, width):
    for axis, dim in sides:
        size, length = (lax.axis_size(axis), array.shape[dim])
        up = [(i, (i + 1) % size) for i in range(size - 1)]
        down = [(j, i) for i, j in up]
        last = lax.slice_in_dim(array, length - width, length, axis=dim)
        leading = lax.slice_in_dim(array, 0, width, axis=dim)
        before = lax.ppermute(last, axis, up)
        after = lax.ppermute(leading, axis, down)
        array = jnp.concatenate([before, array, after], axis=dim)
    return array


def local(wavefunctions, cell_matrix, cell_nodes, home_counts, atom_start, projectors, coupling):
    own_rows, columns = wavefunctions.shape
    cell_width = cell_nodes.shape[1]
    ghost_rows = cell_width // 4
    extended_rows = own_rows + 2 * ghost_rows
    atom_home = coupling.shape[0]
    projector_count = coupling.shape[1]
    support = projectors.shape[-1]
    slot_count = 3 * atom_home
    home_rows = atom_home * projector_count
    starts = atom_start.reshape(slot_count)
    projector_flat = projectors.reshape(slot_count, projector_count, support)
    slot_mask = (
        (lax.broadcasted_iota(jnp.int32, (3, atom_home), 1) < home_counts.reshape(3, 1))
        .astype(jnp.float32)
        .reshape(slot_count)
    )
    slot_rows = starts[:, None] + lax.broadcasted_iota(jnp.int32, (slot_count, support), 1)
    node_list = cell_nodes.reshape(-1)

    def apply_hamiltonian(vector):
        rounded = vector.astype(jnp.bfloat16)
        extended = with_halo(rounded, (("dom", 0),), ghost_rows)
        cell_inputs = extended[cell_nodes]
        products = lax.dot_general(
            cell_matrix,
            cell_inputs,
            (((2,), (1,)), ((0,), (0,))),
            preferred_element_type=jnp.float32,
        )
        assembled = (
            jnp.zeros((extended_rows, columns), jnp.float32)
            .at[node_list]
            .add(products.reshape(-1, columns))
        )
        windows = rounded[slot_rows]
        coefficients = (
            lax.dot_general(
                projector_flat,
                windows,
                (((2,), (1,)), ((0,), (0,))),
                preferred_element_type=jnp.float32,
            )
            * slot_mask[:, None, None]
        )
        slot_table = coefficients.reshape(3, home_rows, columns)
        cell_rims = jnp.concatenate(
            [assembled[:ghost_rows], assembled[extended_rows - ghost_rows :]], 0
        )
        summed = with_halo(cell_rims, (("dom", 0),), ghost_rows)
        left_cells = summed[:ghost_rows]
        right_cells = summed[3 * ghost_rows :]
        slot_rims = jnp.concatenate([slot_table[0], slot_table[2]], 0)
        arrived = with_halo(slot_rims, (("dom", 0),), home_rows)
        left_home = arrived[:home_rows]
        right_home = arrived[3 * home_rows :]
        cell_part = assembled[ghost_rows : ghost_rows + own_rows]
        cell_part = cell_part.at[:ghost_rows].add(left_cells)
        cell_part = cell_part.at[own_rows - ghost_rows :].add(right_cells)
        home_sum = (slot_table[1] + left_home + right_home).reshape(
            atom_home, projector_count, columns
        )
        atom_values = jnp.einsum(
            "apq,aqw->apw", coupling, home_sum, precision=lax.Precision.HIGHEST
        ).astype(jnp.bfloat16)
        nearby = with_halo(atom_values, (("dom", 0),), atom_home)
        contributions = (
            lax.dot_general(
                projector_flat,
                nearby,
                (((1,), (1,)), ((0,), (0,))),
                preferred_element_type=jnp.float32,
            )
            * slot_mask[:, None, None]
        )
        projected_part = (
            jnp.zeros((own_rows, columns), jnp.float32)
            .at[slot_rows.reshape(-1)]
            .add(contributions.reshape(-1, columns))
        )
        return cell_part + projected_part

    half_width = (upper_edge - cut_edge) / 2.0
    centre = (upper_edge + cut_edge) / 2.0
    sigma_one = half_width / (lower_edge - centre)
    gamma_ratio = 2.0 / sigma_one

    def shifted(vector):
        return apply_hamiltonian(vector) - centre * vector

    order_one = shifted(wavefunctions) * (sigma_one / half_width)
    sigma_two = 1.0 / (gamma_ratio - sigma_one)
    order_two = (
        shifted(order_one) * (2.0 * sigma_two / half_width) - sigma_one * sigma_two * wavefunctions
    )
    sigma_three = 1.0 / (gamma_ratio - sigma_two)
    filtered = (
        shifted(order_two) * (2.0 * sigma_three / half_width) - sigma_two * sigma_three * order_one
    )
    block_total = lax.psum(jnp.sum(filtered * filtered), ("dom", "wf"))
    return (filtered, jnp.sqrt(block_total))


def solution(mesh):
    return jax.shard_map(
        local,
        mesh=mesh,
        in_specs=(
            P("dom", "wf"),
            P("dom", None, None),
            P("dom", None),
            P("dom", None),
            P("dom", None, None),
            P("dom", None, None, None, None),
            P("dom", None, None),
        ),
        out_specs=(P("dom", "wf"), P()),
        check_vma=False,
    )
```

profile of v0, /device:TPU:1, one launch (start us, length us, event | category | flops | bytes accessed | tf_op | source)
XLA Modules:
  0.0 346.9 jit_solution(14432529227748252050)
XLA Ops:
  4.3 9.2 %gather_fusion.1 = bf16[3072,128]{1,0:T(8,128)(2,1)S(1)} fusion(bf16[512,128]{1,0:T(8,128)(2,1)S(1)} %convert_element_type.37, s32[3072]{0:T(1024)S(1)} %broadcast_clamp_fusion), kind=kCustom, calls=%fused_computation.1 | custom fusion | bytes 1585152 | tf_op jit(solution)/shard_map/gather | solution.py:59
  13.8 4.5 %collective-permute-start.4 = (f32[72,128]{1,0:T(8,128)S(1)}, f32[72,128]{1,0:T(8,128)S(1)}, u32[]{:S(2)}, u32[]{:S(2)}) collective-permute-start(f32[72,128]{1,0:T(8,128)S(1)} %squeeze.28), channel_id=1, source_target_pairs={{0,24},{24,48},{48,72},{72,96},{96,120},{120,144},{144,168},{168,1... | collective-permute-start | bytes 110600 | tf_op jit(solution)/shard_map/ppermute | solution.py:18
  18.3 9.2 %collective-permute-start.5 = (f32[72,128]{1,0:T(8,128)S(1)}, f32[72,128]{1,0:T(8,128)S(1)}, u32[]{:S(2)}, u32[]{:S(2)}) collective-permute-start(f32[72,128]{1,0:T(8,128)S(1)} %squeeze.29), channel_id=1, source_target_pairs={{24,0},{48,24},{72,48},{96,72},{120,96},{144,120},{168,144},{192,1... | collective-permute-start | bytes 110600 | tf_op jit(solution)/shard_map/ppermute | solution.py:19
  27.5 1.9 collective-permute-start
  29.4 2.4 collective-permute-start.1
  32.6 2.0 collective-permute-done.1
  34.7 3.2 gather_fusion
  38.6 6.1 %scatter_custom_fusion = f32[768,128]{1,0:T(8,128)S(1)} fusion(s32[1024]{0:T(1024)S(1)} %bitcast.97, f32[1024,128]{1,0:T(8,128)S(1)} %bitcast.88, f32[]{:T(128)} %constant.153.clone.1), kind=kCustom, calls=%fused_computation.42 | custom fusion | flops 131072 | bytes 393220 | tf_op jit(solution)/shard_map/scatter-add | solution.py:57
  45.0 1.9 collective-permute-start.6
  47.0 2.4 collective-permute-start.7
  50.0 3.2 collective-permute-start.2
  59.0 17.4 %scatter_fusion = f32[512,128]{1,0:T(8,128)S(1)} fusion(f32[512,128]{1,0:T(8,128)S(1)} %fusion.32, s32[3072]{0:T(1024)} %bitcast.90, f32[3072,128]{1,0:T(8,128)} %bitcast.79), kind=kCustom, calls=%fused_computation.7 | custom fusion | flops 393216 | bytes 4730880 | tf_op jit(solution)/shard_map/scatter-add | solution.py:102
  76.5 9.2 %gather_fusion.3 = bf16[3072,128]{1,0:T(8,128)(2,1)S(1)} fusion(bf16[512,128]{1,0:T(8,128)(2,1)S(1)} %multiply_convert_fusion, s32[3072]{0:T(1024)S(1)} %copy-done.9), kind=kCustom, calls=%fused_computation.3 | custom fusion | bytes 1585152 | tf_op jit(solution)/shard_map/gather | solution.py:59
  85.9 2.6 collective-permute-start.8
  90.5 3.6 %collective-permute-start.12 = (f32[72,128]{1,0:T(8,128)S(1)}, f32[72,128]{1,0:T(8,128)S(1)}, u32[]{:S(2)}, u32[]{:S(2)}) collective-permute-start(f32[72,128]{1,0:T(8,128)S(1)} %squeeze.31), channel_id=1, source_target_pairs={{0,24},{24,48},{48,72},{72,96},{96,120},{120,144},{144,168},{168,1... | collective-permute-start | bytes 110600 | tf_op jit(solution)/shard_map/ppermute | solution.py:18
  96.1 3.2 gather_fusion.2
  100.0 6.2 %scatter_custom_fusion.2 = f32[768,128]{1,0:T(8,128)S(1)} fusion(s32[1024]{0:T(1024)} %bitcast.98, f32[1024,128]{1,0:T(8,128)S(1)} %bitcast.89, f32[]{:T(128)} %constant.153.clone.1), kind=kCustom, calls=%fused_computation.40 | custom fusion | flops 131072 | bytes 393728 | tf_op jit(solution)/shard_map/scatter-add | solution.py:57
  106.6 3.6 %collective-permute-start.14 = (bf16[4,18,128]{2,1,0:T(8,128)(2,1)S(1)}, bf16[4,18,128]{2,1,0:T(8,128)(2,1)S(1)}, u32[]{:S(2)}, u32[]{:S(2)}) collective-permute-start(bf16[4,18,128]{2,1,0:T(8,128)(2,1)S(1)} %fusion.4), channel_id=1, source_target_pairs={{0,24},{24,48},{48,72},{72,96},{96,120},{120,144},{144,168},{168,1... | collective-permute-start | bytes 55304 | tf_op jit(solution)/shard_map/ppermute | solution.py:18
  112.8 3.6 %collective-permute-start.10 = (f32[128,128]{1,0:T(8,128)}, f32[128,128]{1,0:T(8,128)}, u32[]{:S(2)}, u32[]{:S(2)}) collective-permute-start(f32[128,128]{1,0:T(8,128)} %get-tuple-element.79), channel_id=1, source_target_pairs={{0,24},{24,48},{48,72},{72,96},{96,120},{120,144},{144,168},{168,1... | collective-permute-start | bytes 196616 | tf_op jit(solution)/shard_map/ppermute | solution.py:18
  116.5 1.9 collective-permute-start.11
  123.3 17.5 %scatter_fusion.1 = f32[512,128]{1,0:T(8,128)S(1)} fusion(f32[512,128]{1,0:T(8,128)S(1)} %fusion.30, s32[3072]{0:T(1024)} %bitcast.91, f32[3072,128]{1,0:T(8,128)} %bitcast.80), kind=kCustom, calls=%fused_computation.9 | custom fusion | flops 393216 | bytes 4730880 | tf_op jit(solution)/shard_map/scatter-add | solution.py:102
  140.9 9.2 %gather_fusion.5 = bf16[3072,128]{1,0:T(8,128)(2,1)S(1)} fusion(bf16[512,128]{1,0:T(8,128)(2,1)S(1)} %fusion.27, s32[3072]{0:T(1024)S(1)} %copy-done.10), kind=kCustom, calls=%fused_computation.5 | custom fusion | bytes 1585152 | tf_op jit(solution)/shard_map/gather | solution.py:59
  150.3 3.3 collective-permute-start.16
  155.7 3.6 %collective-permute-start.20 = (f32[72,128]{1,0:T(8,128)S(1)}, f32[72,128]{1,0:T(8,128)S(1)}, u32[]{:S(2)}, u32[]{:S(2)}) collective-permute-start(f32[72,128]{1,0:T(8,128)S(1)} %squeeze.34), channel_id=1, source_target_pairs={{0,24},{24,48},{48,72},{72,96},{96,120},{120,144},{144,168},{168,1... | collective-permute-start | bytes 110600 | tf_op jit(solution)/shard_map/ppermute | solution.py:18
  161.3 3.2 gather_fusion.4
  165.2 6.2 %scatter_custom_fusion.4 = f32[768,128]{1,0:T(8,128)S(1)} fusion(s32[1024]{0:T(1024)} %bitcast.99, f32[1024,128]{1,0:T(8,128)S(1)} %bitcast.87, f32[]{:T(128)} %constant.153.clone.1), kind=kCustom, calls=%fused_computation.38 | custom fusion | flops 131072 | bytes 393728 | tf_op jit(solution)/shard_map/scatter-add | solution.py:57
  171.8 3.6 %collective-permute-start.22 = (bf16[4,18,128]{2,1,0:T(8,128)(2,1)S(1)}, bf16[4,18,128]{2,1,0:T(8,128)(2,1)S(1)}, u32[]{:S(2)}, u32[]{:S(2)}) collective-permute-start(bf16[4,18,128]{2,1,0:T(8,128)(2,1)S(1)} %fusion.5), channel_id=1, source_target_pairs={{0,24},{24,48},{48,72},{72,96},{96,120},{120,144},{144,168},{168,1... | collective-permute-start | bytes 55304 | tf_op jit(solution)/shard_map/ppermute | solution.py:18
  175.4 1.9 collective-permute-start.23
  178.0 6.0 %collective-permute-start.18 = (f32[128,128]{1,0:T(8,128)}, f32[128,128]{1,0:T(8,128)}, u32[]{:S(2)}, u32[]{:S(2)}) collective-permute-start(f32[128,128]{1,0:T(8,128)} %get-tuple-element.77), channel_id=1, source_target_pairs={{0,24},{24,48},{48,72},{72,96},{96,120},{120,144},{144,168},{168,1... | collective-permute-start | bytes 196616 | tf_op jit(solution)/shard_map/ppermute | solution.py:18
  184.0 1.9 collective-permute-start.19
  191.7 17.4 %scatter_fusion.2 = f32[512,128]{1,0:T(8,128)S(1)} fusion(f32[512,128]{1,0:T(8,128)S(1)} %fusion.28, s32[3072]{0:T(1024)S(1)} %bitcast.92, f32[3072,128]{1,0:T(8,128)} %bitcast.78), kind=kCustom, calls=%fused_computation.11 | custom fusion | flops 393216 | bytes 4730880 | tf_op jit(solution)/shard_map/scatter-add | solution.py:102
  210.6 134.5 %psum.7 = f32[]{:T(128)} all-reduce(f32[]{:T(128)} %get-tuple-element.74), channel_id=1, replica_groups=mesh['dom'=32,'wf'=24] {'dom','wf'}, use_global_device_ids=true, to_apply=%region_7.0 | all-reduce | flops 1 | bytes 8 | tf_op jit(solution)/shard_map/psum | solution.py:123
  (143 shorter events, 37.4 us)
Async XLA Ops:
  0.6 37.3 %copy-start = (bf16[2,512,512]{2,1,0:T(8,128)(2,1)S(1)}, bf16[2,512,512]{2,1,0:T(8,128)(2,1)}, u32[]{:S(2)}) copy-start(bf16[2,512,512]{2,1,0:T(8,128)(2,1)} %param.20) | copy-start | bytes 3145732
  13.5 18.4 %copy-start.18 = (s32[2,512]{1,0:T(2,128)S(1)}, s32[2,512]{1,0:T(2,128)}, u32[]{:S(2)}) copy-start(s32[2,512]{1,0:T(2,128)} %param.21) | copy-start | bytes 12292
  13.8 31.0 %collective-permute-start.4 = (f32[72,128]{1,0:T(8,128)S(1)}, f32[72,128]{1,0:T(8,128)S(1)}, u32[]{:S(2)}, u32[]{:S(2)}) collective-permute-start(f32[72,128]{1,0:T(8,128)S(1)} %squeeze.28), channel_id=1, source_target_pairs={{0,24},{24,48},{48,72},{72,96},{96,120},{120,144},{144,168},{168,1... | collective-permute-start | bytes 110600 | tf_op jit(solution)/shard_map/ppermute | solution.py:18
  18.3 26.5 %collective-permute-start.5 = (f32[72,128]{1,0:T(8,128)S(1)}, f32[72,128]{1,0:T(8,128)S(1)}, u32[]{:S(2)}, u32[]{:S(2)}) collective-permute-start(f32[72,128]{1,0:T(8,128)S(1)} %squeeze.29), channel_id=1, source_target_pairs={{24,0},{48,24},{72,48},{96,72},{120,96},{144,120},{168,144},{192,1... | collective-permute-start | bytes 110600 | tf_op jit(solution)/shard_map/ppermute | solution.py:19
  27.5 5.1 %collective-permute-start = (bf16[128,128]{1,0:T(8,128)(2,1)S(1)}, bf16[128,128]{1,0:T(8,128)(2,1)S(1)}, u32[]{:S(2)}, u32[]{:S(2)}) collective-permute-start(bf16[128,128]{1,0:T(8,128)(2,1)S(1)} %get-tuple-element.95), channel_id=1, source_target_pairs={{0,24},{24,48},{48,72},{72,96},{96,120},{120,144},{144,168},{168,1... | collective-permute-start | bytes 98312 | tf_op jit(solution)/shard_map/ppermute | solution.py:18
  29.4 5.2 %collective-permute-start.1 = (bf16[128,128]{1,0:T(8,128)(2,1)S(1)}, bf16[128,128]{1,0:T(8,128)(2,1)S(1)}, u32[]{:S(2)}, u32[]{:S(2)}) collective-permute-start(bf16[128,128]{1,0:T(8,128)(2,1)S(1)} %get-tuple-element.96), channel_id=1, source_target_pairs={{24,0},{48,24},{72,48},{96,72},{120,96},{144,120},{168,144},{192,1... | collective-permute-start | bytes 98312 | tf_op jit(solution)/shard_map/ppermute | solution.py:19
  45.0 10.1 %collective-permute-start.6 = (bf16[4,18,128]{2,1,0:T(8,128)(2,1)S(1)}, bf16[4,18,128]{2,1,0:T(8,128)(2,1)S(1)}, u32[]{:S(2)}, u32[]{:S(2)}) collective-permute-start(bf16[4,18,128]{2,1,0:T(8,128)(2,1)S(1)} %fusion.3), channel_id=1, source_target_pairs={{0,24},{24,48},{48,72},{72,96},{96,120},{120,144},{144,168},{168,1... | collective-permute-start | bytes 55304 | tf_op jit(solution)/shard_map/ppermute | solution.py:18
  47.0 8.2 %collective-permute-start.7 = (bf16[4,18,128]{2,1,0:T(8,128)(2,1)S(1)}, bf16[4,18,128]{2,1,0:T(8,128)(2,1)S(1)}, u32[]{:S(2)}, u32[]{:S(2)}) collective-permute-start(bf16[4,18,128]{2,1,0:T(8,128)(2,1)S(1)} %fusion.3), channel_id=1, source_target_pairs={{24,0},{48,24},{72,48},{96,72},{120,96},{144,120},{168,144},{192,1... | collective-permute-start | bytes 55304 | tf_op jit(solution)/shard_map/ppermute | solution.py:19
  50.0 7.9 %collective-permute-start.2 = (f32[128,128]{1,0:T(8,128)}, f32[128,128]{1,0:T(8,128)S(1)}, u32[]{:S(2)}, u32[]{:S(2)}) collective-permute-start(f32[128,128]{1,0:T(8,128)} %get-tuple-element.81), channel_id=1, source_target_pairs={{0,24},{24,48},{48,72},{72,96},{96,120},{120,144},{144,168},{168,1... | collective-permute-start | bytes 196616 | tf_op jit(solution)/shard_map/ppermute | solution.py:18
  53.2 5.8 %collective-permute-start.3 = (f32[128,128]{1,0:T(8,128)}, f32[128,128]{1,0:T(8,128)S(1)}, u32[]{:S(2)}, u32[]{:S(2)}) collective-permute-start(f32[128,128]{1,0:T(8,128)} %get-tuple-element.80), channel_id=1, source_target_pairs={{24,0},{48,24},{72,48},{96,72},{120,96},{144,120},{168,144},{192,1... | collective-permute-start | bytes 196616 | tf_op jit(solution)/shard_map/ppermute | solution.py:19
  59.0 17.4 %copy-start.1 = (f32[512,128]{1,0:T(8,128)S(1)}, f32[512,128]{1,0:T(8,128)}, u32[]{:S(2)}) copy-start(f32[512,128]{1,0:T(8,128)} %param.19) | copy-start | bytes 786436
  59.0 17.5 %copy-start.9 = (s32[3072]{0:T(1024)S(1)}, s32[3072]{0:T(1024)}, u32[]{:S(2)}) copy-start(s32[3072]{0:T(1024)} %copy-done.8) | copy-start | bytes 36868
  85.9 10.1 %collective-permute-start.8 = (bf16[128,128]{1,0:T(8,128)(2,1)S(1)}, bf16[128,128]{1,0:T(8,128)(2,1)S(1)}, u32[]{:S(2)}, u32[]{:S(2)}) collective-permute-start(bf16[128,128]{1,0:T(8,128)(2,1)S(1)} %get-tuple-element.93), channel_id=1, source_target_pairs={{0,24},{24,48},{48,72},{72,96},{96,120},{120,144},{144,168},{168,1... | collective-permute-start | bytes 98312 | tf_op jit(solution)/shard_map/ppermute | solution.py:18
  88.5 7.6 %collective-permute-start.9 = (bf16[128,128]{1,0:T(8,128)(2,1)S(1)}, bf16[128,128]{1,0:T(8,128)(2,1)S(1)}, u32[]{:S(2)}, u32[]{:S(2)}) collective-permute-start(bf16[128,128]{1,0:T(8,128)(2,1)S(1)} %get-tuple-element.94), channel_id=1, source_target_pairs={{24,0},{48,24},{72,48},{96,72},{120,96},{144,120},{168,144},{192,1... | collective-permute-start | bytes 98312 | tf_op jit(solution)/shard_map/ppermute | solution.py:19
  90.5 15.8 %collective-permute-start.12 = (f32[72,128]{1,0:T(8,128)S(1)}, f32[72,128]{1,0:T(8,128)S(1)}, u32[]{:S(2)}, u32[]{:S(2)}) collective-permute-start(f32[72,128]{1,0:T(8,128)S(1)} %squeeze.31), channel_id=1, source_target_pairs={{0,24},{24,48},{48,72},{72,96},{96,120},{120,144},{144,168},{168,1... | collective-permute-start | bytes 110600 | tf_op jit(solution)/shard_map/ppermute | solution.py:18
  94.1 12.2 %collective-permute-start.13 = (f32[72,128]{1,0:T(8,128)S(1)}, f32[72,128]{1,0:T(8,128)S(1)}, u32[]{:S(2)}, u32[]{:S(2)}) collective-permute-start(f32[72,128]{1,0:T(8,128)S(1)} %squeeze.32), channel_id=1, source_target_pairs={{24,0},{48,24},{72,48},{96,72},{120,96},{144,120},{168,144},{192,1... | collective-permute-start | bytes 110600 | tf_op jit(solution)/shard_map/ppermute | solution.py:19
  106.3 12.1 %copy-start.4 = (f32[768,128]{1,0:T(8,128)}, f32[768,128]{1,0:T(8,128)S(1)}, u32[]{:S(2)}) copy-start(f32[768,128]{1,0:T(8,128)S(1)} %scatter_custom_fusion.2) | copy-start | bytes 1179652
  106.6 11.8 %collective-permute-start.14 = (bf16[4,18,128]{2,1,0:T(8,128)(2,1)S(1)}, bf16[4,18,128]{2,1,0:T(8,128)(2,1)S(1)}, u32[]{:S(2)}, u32[]{:S(2)}) collective-permute-start(bf16[4,18,128]{2,1,0:T(8,128)(2,1)S(1)} %fusion.4), channel_id=1, source_target_pairs={{0,24},{24,48},{48,72},{72,96},{96,120},{120,144},{144,168},{168,1... | collective-permute-start | bytes 55304 | tf_op jit(solution)/shard_map/ppermute | solution.py:18
  110.2 8.2 %collective-permute-start.15 = (bf16[4,18,128]{2,1,0:T(8,128)(2,1)S(1)}, bf16[4,18,128]{2,1,0:T(8,128)(2,1)S(1)}, u32[]{:S(2)}, u32[]{:S(2)}) collective-permute-start(bf16[4,18,128]{2,1,0:T(8,128)(2,1)S(1)} %fusion.4), channel_id=1, source_target_pairs={{24,0},{48,24},{72,48},{96,72},{120,96},{144,120},{168,144},{192,1... | collective-permute-start | bytes 55304 | tf_op jit(solution)/shard_map/ppermute | solution.py:19
  112.8 8.4 %collective-permute-start.10 = (f32[128,128]{1,0:T(8,128)}, f32[128,128]{1,0:T(8,128)}, u32[]{:S(2)}, u32[]{:S(2)}) collective-permute-start(f32[128,128]{1,0:T(8,128)} %get-tuple-element.79), channel_id=1, source_target_pairs={{0,24},{24,48},{48,72},{72,96},{96,120},{120,144},{144,168},{168,1... | collective-permute-start | bytes 196616 | tf_op jit(solution)/shard_map/ppermute | solution.py:18
  116.5 5.9 %collective-permute-start.11 = (f32[128,128]{1,0:T(8,128)}, f32[128,128]{1,0:T(8,128)}, u32[]{:S(2)}, u32[]{:S(2)}) collective-permute-start(f32[128,128]{1,0:T(8,128)} %get-tuple-element.78), channel_id=1, source_target_pairs={{24,0},{48,24},{72,48},{96,72},{120,96},{144,120},{168,144},{192,1... | collective-permute-start | bytes 196616 | tf_op jit(solution)/shard_map/ppermute | solution.py:19
  123.2 17.7 %copy-start.10 = (s32[3072]{0:T(1024)S(1)}, s32[3072]{0:T(1024)}, u32[]{:S(2)}) copy-start(s32[3072]{0:T(1024)} %copy-done.8) | copy-start | bytes 36868
  150.3 10.9 %collective-permute-start.16 = (bf16[128,128]{1,0:T(8,128)(2,1)S(1)}, bf16[128,128]{1,0:T(8,128)(2,1)S(1)}, u32[]{:S(2)}, u32[]{:S(2)}) collective-permute-start(bf16[128,128]{1,0:T(8,128)(2,1)S(1)} %get-tuple-element.91), channel_id=1, source_target_pairs={{0,24},{24,48},{48,72},{72,96},{96,120},{120,144},{144,168},{168,1... | collective-permute-start | bytes 98312 | tf_op jit(solution)/shard_map/ppermute | solution.py:18
  153.7 7.6 %collective-permute-start.17 = (bf16[128,128]{1,0:T(8,128)(2,1)S(1)}, bf16[128,128]{1,0:T(8,128)(2,1)S(1)}, u32[]{:S(2)}, u32[]{:S(2)}) collective-permute-start(bf16[128,128]{1,0:T(8,128)(2,1)S(1)} %get-tuple-element.92), channel_id=1, source_target_pairs={{24,0},{48,24},{72,48},{96,72},{120,96},{144,120},{168,144},{192,1... | collective-permute-start | bytes 98312 | tf_op jit(solution)/shard_map/ppermute | solution.py:19
  155.7 15.8 %collective-permute-start.20 = (f32[72,128]{1,0:T(8,128)S(1)}, f32[72,128]{1,0:T(8,128)S(1)}, u32[]{:S(2)}, u32[]{:S(2)}) collective-permute-start(f32[72,128]{1,0:T(8,128)S(1)} %squeeze.34), channel_id=1, source_target_pairs={{0,24},{24,48},{48,72},{72,96},{96,120},{120,144},{144,168},{168,1... | collective-permute-start | bytes 110600 | tf_op jit(solution)/shard_map/ppermute | solution.py:18
  159.3 12.2 %collective-permute-start.21 = (f32[72,128]{1,0:T(8,128)S(1)}, f32[72,128]{1,0:T(8,128)S(1)}, u32[]{:S(2)}, u32[]{:S(2)}) collective-permute-start(f32[72,128]{1,0:T(8,128)S(1)} %squeeze.35), channel_id=1, source_target_pairs={{24,0},{48,24},{72,48},{96,72},{120,96},{144,120},{168,144},{192,1... | collective-permute-start | bytes 110600 | tf_op jit(solution)/shard_map/ppermute | solution.py:19
  171.5 14.5 %copy-start.3 = (f32[768,128]{1,0:T(8,128)}, f32[768,128]{1,0:T(8,128)S(1)}, u32[]{:S(2)}) copy-start(f32[768,128]{1,0:T(8,128)S(1)} %scatter_custom_fusion.4) | copy-start | bytes 1179652
  171.8 14.2 %collective-permute-start.22 = (bf16[4,18,128]{2,1,0:T(8,128)(2,1)S(1)}, bf16[4,18,128]{2,1,0:T(8,128)(2,1)S(1)}, u32[]{:S(2)}, u32[]{:S(2)}) collective-permute-start(bf16[4,18,128]{2,1,0:T(8,128)(2,1)S(1)} %fusion.5), channel_id=1, source_target_pairs={{0,24},{24,48},{48,72},{72,96},{96,120},{120,144},{144,168},{168,1... | collective-permute-start | bytes 55304 | tf_op jit(solution)/shard_map/ppermute | solution.py:18
  175.4 10.5 %collective-permute-start.23 = (bf16[4,18,128]{2,1,0:T(8,128)(2,1)S(1)}, bf16[4,18,128]{2,1,0:T(8,128)(2,1)S(1)}, u32[]{:S(2)}, u32[]{:S(2)}) collective-permute-start(bf16[4,18,128]{2,1,0:T(8,128)(2,1)S(1)} %fusion.5), channel_id=1, source_target_pairs={{24,0},{48,24},{72,48},{96,72},{120,96},{144,120},{168,144},{192,1... | collective-permute-start | bytes 55304 | tf_op jit(solution)/shard_map/ppermute | solution.py:19
  178.0 10.7 %collective-permute-start.18 = (f32[128,128]{1,0:T(8,128)}, f32[128,128]{1,0:T(8,128)}, u32[]{:S(2)}, u32[]{:S(2)}) collective-permute-start(f32[128,128]{1,0:T(8,128)} %get-tuple-element.77), channel_id=1, source_target_pairs={{0,24},{24,48},{48,72},{72,96},{96,120},{120,144},{144,168},{168,1... | collective-permute-start | bytes 196616 | tf_op jit(solution)/shard_map/ppermute | solution.py:18
  184.0 6.8 %collective-permute-start.19 = (f32[128,128]{1,0:T(8,128)}, f32[128,128]{1,0:T(8,128)}, u32[]{:S(2)}, u32[]{:S(2)}) collective-permute-start(f32[128,128]{1,0:T(8,128)} %get-tuple-element.76), channel_id=1, source_target_pairs={{24,0},{48,24},{72,48},{96,72},{120,96},{144,120},{168,144},{192,1... | collective-permute-start | bytes 196616 | tf_op jit(solution)/shard_map/ppermute | solution.py:19
  191.7 17.4 %copy-start.2 = (f32[512,128]{1,0:T(8,128)S(1)}, f32[512,128]{1,0:T(8,128)}, u32[]{:S(2)}) copy-start(f32[512,128]{1,0:T(8,128)} %param.19) | copy-start | bytes 786436
  (12 other events, 98.6 us)
where the time goes:
time: 348 us; the launch traced here: 347 us
  blocking collectives  135 us (39%)
  other arithmetic  79.3 us (23%)
  starting transfers between devices  72.9 us (21%)
  local copies, waits for them, and re-layouts  46 us (13%)
  matrix products  5.99 us (2%)
  waiting for transfers between devices  4.73 us (1%)
  between operations  3.56 us (1%)
    psum x1, blocking collectives, local(): block_total = lax.psum(jnp.sum(filtered * filtered), ('dom', 'wf'))  135 us
    scatter-add x3, other arithmetic, apply_hamiltonian(): projected_part = jnp.zeros((own_rows, columns), jnp.float32).at[slot_rows...  52.3 us
    ppermute x12, starting transfers between devices, with_halo(): before = lax.ppermute(last, axis, up)  41.6 us
    ppermute x12, starting transfers between devices, with_halo(): after = lax.ppermute(leading, axis, down)  31.3 us
    gather x3, local copies, waits for them, and re-layouts, apply_hamiltonian(): windows = rounded[slot_rows]  27.5 us
    scatter-add x3, other arithmetic, apply_hamiltonian(): assembled = jnp.zeros((extended_rows, columns), jnp.float32).at[node_list...  18.6 us
    gather x3, local copies, waits for them, and re-layouts, apply_hamiltonian(): cell_inputs = extended[cell_nodes]  9.63 us
  transfers between devices with their start and end apart: 24, of which 4 were waited for; matrix products, arithmetic and copies ran while one was open for 12% of the time, Pallas kernels for 0%

commit v1 on v0

v1 whole, which is shorter than its diff:
```python
import functools

import jax
import jax.numpy as jnp
from jax import lax
from jax.experimental import pallas as pl
from jax.experimental.pallas import tpu as pltpu
from jax.sharding import PartitionSpec as P

F32, BF16 = jnp.float32, jnp.bfloat16
MESH = pl.DeviceIdType.MESH

lower_edge = -1.0
cut_edge = 2.0
upper_edge = 9.0

CELLS = 2
NPC = 512
OWN = 512
GHOST = 128
EXT = OWN + 2 * GHOST
COLS = 128
NPROJ, SUP, ATOM_HOME = 18, 256, 4
SLOT = 24
HOME = 80
PROWS = 3 * HOME
GROWS = 2 * GHOST + PROWS
BLK = GHOST + 2 * HOME
LO = GHOST + PROWS
ROW, PLANE, ZLO = 8, 3, 4


def dot(a, b):
    return jnp.dot(a, b, preferred_element_type=F32)


def dot_nt(a, b):
    return lax.dot_general(a, b, (((1,), (1,)), ((), ())), preferred_element_type=F32)


def dot_tn(a, b):
    return lax.dot_general(a, b, (((0,), (0,)), ((), ())), preferred_element_type=F32)


def kernel(
    ny,
    wave_ref, matrix_ref, nodes_ref, counts_ref, starts_ref, proj_ref, coupling_ref,
    out_ref, norm_ref,
    fv, vb, gb, xb, rblk, rc2, c32, acc,
    cm, scat, tcat, gmat, ahi, alo, fmat, corner, csend, crecv,
    pin, pst, pall, cin, cst, csn, crc, call,
    part, ysum, zsum,
    in_sem, out_sem, send_sem, recv_sem, ssend_sem, srecv_sem,
    nsend, nrecv,
):
    d, w = lax.axis_index("dom"), lax.axis_index("wf")
    n_dom = 32
    below1, below2, above1, above2 = d >= 1, d >= 2, d < n_dom - 1, d < n_dom - 2

    loads = [
        pltpu.make_async_copy(proj_ref, pin, in_sem.at[0]),
        pltpu.make_async_copy(coupling_ref, cin, in_sem.at[1]),
        pltpu.make_async_copy(matrix_ref, cm, in_sem.at[2]),
        pltpu.make_async_copy(wave_ref, fv.at[0], in_sem.at[3]),
    ]
    for load in loads:
        load.start()

    zlo, row = lax.div(d, ROW), lax.rem(d, ROW)
    y, zhi = lax.div(w, PLANE), lax.rem(w, PLANE)
    z = zhi * ZLO + zlo
    nz = ZLO * PLANE

    def row_peer(k):
        i = lax.rem(row + k, ROW)
        return i, (zlo * ROW + i, w)

    def y_peer(k):
        i = lax.rem(y + k, ny)
        return i, (d, i * PLANE + zhi)

    def z_peer(k):
        i = lax.rem(z + k, nz)
        return i, (lax.rem(i, ZLO) * ROW + row, y * PLANE + lax.div(i, ZLO))

    stages = ((ROW, row_peer, row), (ny, y_peer, y), (nz, z_peer, z))

    barrier = pltpu.get_barrier_semaphore()
    for cond, other in ((below1, d - 1), (above1, d + 1), (below2, d - 2), (above2, d + 2)):
        @pl.when(cond)
        def _():
            pl.semaphore_signal(barrier, inc=1, device_id=(other, w), device_id_type=MESH)
    for size, peer, _ in stages:
        for k in range(1, size):
            pl.semaphore_signal(barrier, inc=1, device_id=peer(k)[1], device_id_type=MESH)

    def zero(ref):
        ref[...] = jnp.zeros(ref.shape, ref.dtype)

    for a in range(3):
        zero(xb.at[a, pl.ds(OWN, EXT - OWN)])
    for cond, refs in (
        (below1, lambda: [rblk.at[a, 0] for a in range(3)] + [xb.at[a, pl.ds(GHOST, GHOST)] for a in range(3)] + [crecv.at[0], crc.at[0]]),
        (above1, lambda: [rblk.at[a, 1] for a in range(3)] + [xb.at[a, pl.ds(2 * GHOST, GHOST)] for a in range(3)] + [crecv.at[1], crc.at[1]]),
        (below2, lambda: [rc2.at[a, 0] for a in range(3)] + [xb.at[a, pl.ds(0, GHOST)] for a in range(3)]),
        (above2, lambda: [rc2.at[a, 1] for a in range(3)] + [xb.at[a, pl.ds(3 * GHOST, GHOST)] for a in range(3)]),
    ):
        @pl.when(jnp.logical_not(cond))
        def _():
            for ref in refs():
                zero(ref)
    zero(pst)
    zero(cst)
    zero(fmat.at[pl.ds(GHOST, OWN - GHOST), pl.ds(0, GHOST)])
    zero(fmat.at[pl.ds(0, OWN - GHOST), pl.ds(3 * GHOST, GHOST)])

    for c in range(CELLS):
        nodes = nodes_ref[pl.ds(c, 1), :]
        rows = lax.broadcasted_iota(jnp.int32, (EXT, NPC), 0)
        scat[:, c * NPC:(c + 1) * NPC] = jnp.where(rows == nodes, 1.0, 0.0).astype(BF16)

    loads[0].wait()
    for k in range(3):
        for j in range(ATOM_HOME):
            i = (k * ATOM_HOME + j) * SLOT
            pst[pl.ds(i, NPROJ), pl.ds(0, SUP)] = pin[0, k, j].astype(F32)
            live = jnp.where(j < counts_ref[0, k], 1.0, 0.0).astype(F32)
            placed = pltpu.roll(pst[pl.ds(i, SLOT), :], starts_ref[0, k, j], axis=1)
            pst[pl.ds(i, SLOT), :] = placed * live
    pall[...] = pst[...].astype(BF16)
    col = lax.broadcasted_iota(jnp.int32, (1, 3 * ATOM_HOME * SLOT), 1)
    slot, p = lax.div(col, SLOT), lax.rem(col, SLOT)
    target = lax.div(slot, ATOM_HOME) * HOME + lax.rem(slot, ATOM_HOME) * NPROJ + p
    target = jnp.where(p < NPROJ, target, -1)
    pick = jnp.where(
        lax.broadcasted_iota(jnp.int32, (PROWS, 3 * ATOM_HOME * SLOT), 0) == target, 1.0, 0.0
    ).astype(BF16)
    gmat[pl.ds(GHOST, PROWS), :] = dot(pick, pall[...]).astype(BF16)

    loads[1].wait()
    for j in range(ATOM_HOME):
        cst[pl.ds(j * SLOT, NPROJ), pl.ds(0, NPROJ)] = cin[j]
        rows = cst[pl.ds(j * SLOT, SLOT), :]
        csn[pl.ds(j * SLOT, SLOT), :] = rows if j == 0 else pltpu.roll(rows, j * NPROJ, axis=1)

    loads[2].wait()

    def assemble(start, rows):
        for c in range(CELLS):
            tcat[pl.ds(start, rows), c * NPC:(c + 1) * NPC] = dot(
                scat[pl.ds(start, rows), c * NPC:(c + 1) * NPC], cm[c]
            ).astype(BF16)
        return dot_nt(tcat[pl.ds(start, rows), :], scat[...])

    for side, start, grow in ((0, 0, 0), (1, GHOST + OWN, LO)):
        rim = assemble(start, GHOST)
        gmat[pl.ds(grow, GHOST), :] = rim[:, GHOST:GHOST + OWN].astype(BF16)
        csend[side, :, 0:GHOST] = rim[:, 0:GHOST].astype(BF16)
        csend[side, :, GHOST:2 * GHOST] = rim[:, GHOST + OWN:].astype(BF16)

    loads[3].wait()
    vb[0] = fv[0].astype(BF16)

    def remote(src, dst, sems, other):
        return pltpu.make_async_remote_copy(
            src_ref=src, dst_ref=dst, send_sem=sems[0], recv_sem=sems[1],
            device_id=(other, w), device_id_type=MESH,
        )

    def app_copies(a):
        def sems(i):
            return send_sem.at[a, i], recv_sem.at[a, i]

        low, high = vb.at[a, pl.ds(0, GHOST)], vb.at[a, pl.ds(OWN - GHOST, GHOST)]
        edges = [
            (above1, below1, high, xb.at[a, pl.ds(GHOST, GHOST)], sems(0), d + 1),
            (below1, above1, low, xb.at[a, pl.ds(2 * GHOST, GHOST)], sems(4), d - 1),
            (above2, below2, high, xb.at[a, pl.ds(0, GHOST)], sems(2), d + 2),
            (below2, above2, low, xb.at[a, pl.ds(3 * GHOST, GHOST)], sems(6), d - 2),
        ]
        blocks = [
            (above1, below1, gb.at[a, pl.ds(GHOST + HOME, BLK)], rblk.at[a, 0], sems(1), d + 1),
            (below1, above1, gb.at[a, pl.ds(0, BLK)], rblk.at[a, 1], sems(5), d - 1),
            (above2, below2, gb.at[a, pl.ds(GHOST + 2 * HOME, HOME)], rc2.at[a, 0], sems(3), d + 2),
            (below2, above2, gb.at[a, pl.ds(GHOST, HOME)], rc2.at[a, 1], sems(7), d - 2),
        ]
        return edges, blocks

    def setup_copies():
        def sems(i):
            return ssend_sem.at[i], srecv_sem.at[i]

        return [
            (above1, below1, csend.at[1], crecv.at[0], sems(0), d + 1),
            (below1, above1, csend.at[0], crecv.at[1], sems(1), d - 1),
            (above1, below1, csn, crc.at[0], sems(2), d + 1),
            (below1, above1, csn, crc.at[1], sems(3), d - 1),
        ]

    def start(copies):
        for cond, _, src, dst, sems, other in copies:
            @pl.when(cond)
            def _():
                remote(src, dst, sems, other).start()

    def wait_recv(copies):
        for _, cond, src, dst, sems, other in copies:
            @pl.when(cond)
            def _():
                remote(src, dst, sems, other).wait_recv()

    def wait_send(copies):
        for cond, _, src, dst, sems, other in copies:
            @pl.when(cond)
            def _():
                remote(src, dst, sems, other).wait_send()

    def project(a):
        g = dot(gmat[...], vb[a])
        gb[a] = g.astype(BF16)
        c32[...] = g[GHOST:LO]

    project(0)

    pl.semaphore_wait(
        barrier,
        (ROW + ny + nz - 3) + below1.astype(jnp.int32) + below2.astype(jnp.int32)
        + above1.astype(jnp.int32) + above2.astype(jnp.int32),
    )
    for group in app_copies(0):
        start(group)
    start(setup_copies())

    def split(block, rows, cols):
        high = block.astype(BF16)
        ahi[rows, cols] = high
        alo[rows, cols] = (block - high.astype(F32)).astype(BF16)

    for q in range(4):
        rows = pl.ds(q * GHOST, GHOST)
        body = assemble((q + 1) * GHOST, GHOST)
        split(body[:, GHOST:GHOST + OWN], rows, pl.ds(0, OWN))
        if q == 0:
            corner[0] = body[:, GHOST:2 * GHOST]
        if q == 3:
            corner[1] = body[:, OWN:OWN + GHOST]
        fmat[rows, GHOST:2 * GHOST] = body[:, 0:GHOST].astype(BF16)
        fmat[rows, 2 * GHOST:3 * GHOST] = body[:, GHOST + OWN:].astype(BF16)

    wait_recv(setup_copies())
    fmat[0:GHOST, 0:GHOST] = crecv[0, :, 0:GHOST]
    fmat[OWN - GHOST:, 3 * GHOST:4 * GHOST] = crecv[1, :, GHOST:]
    low, high = pl.ds(0, GHOST), pl.ds(OWN - GHOST, GHOST)
    split(corner[0] + crecv[0, :, GHOST:].astype(F32), low, low)
    split(corner[1] + crecv[1, :, 0:GHOST].astype(F32), high, high)
    empty = jnp.zeros((ATOM_HOME * SLOT, 128), F32)
    for k, block in ((0, crc[0]), (1, csn[...]), (2, crc[1])):
        wide = jnp.concatenate([block, empty], axis=1)
        call[pl.ds(k * ATOM_HOME * SLOT, ATOM_HOME * SLOT), :] = wide if k == 0 else pltpu.roll(wide, k * HOME, axis=1)
    couple = call[...]
    couple_hi = couple.astype(BF16)
    couple_lo = (couple - couple_hi.astype(F32)).astype(BF16)
    fmat[:, OWN:] = (dot_tn(pall[...], couple_hi) + dot_tn(pall[...], couple_lo)).astype(BF16)

    half_width = (upper_edge - cut_edge) / 2.0
    centre = (upper_edge + cut_edge) / 2.0
    sigma_one = half_width / (lower_edge - centre)
    gamma_ratio = 2.0 / sigma_one
    sigma_two = 1.0 / (gamma_ratio - sigma_one)
    sigma_three = 1.0 / (gamma_ratio - sigma_two)
    scales = (sigma_one / half_width, 2.0 * sigma_two / half_width, 2.0 * sigma_three / half_width)
    backs = (0.0, sigma_one * sigma_two, sigma_two * sigma_three)

    for a in range(3):
        edges, blocks = app_copies(a)
        if a > 0:
            start(edges)
            project(a)
            start(blocks)
        acc[...] = dot(ahi[...], vb[a]) + dot(alo[...], vb[a]) - centre * fv[a]
        wait_recv(edges)
        wait_recv(blocks)
        below, above = rblk[a, 0].astype(F32), rblk[a, 1].astype(F32)
        own = c32[...]
        xb[a, OWN:OWN + HOME, :] = (own[0:HOME] + below[0:HOME] + rc2[a, 0].astype(F32)).astype(BF16)
        xb[a, OWN + HOME:OWN + 2 * HOME, :] = (
            own[HOME:2 * HOME] + below[HOME:2 * HOME] + above[GHOST:GHOST + HOME]
        ).astype(BF16)
        xb[a, OWN + 2 * HOME:OWN + 3 * HOME, :] = (
            own[2 * HOME:] + above[GHOST + HOME:] + rc2[a, 1].astype(F32)
        ).astype(BF16)
        acc[0:GHOST, :] += below[2 * HOME:]
        acc[OWN - GHOST:, :] += above[0:GHOST]
        new = (acc[...] + dot(fmat[...], xb[a])) * scales[a]
        if a > 0:
            new = new - backs[a] * fv[a - 1]
        fv[a + 1] = new
        if a < 2:
            vb[a + 1] = new.astype(BF16)

    result = fv.at[3]
    store = pltpu.make_async_copy(result, out_ref, out_sem)
    store.start()

    mine = jnp.sum(fv[3] * fv[3], axis=0, keepdims=True)
    base = 0
    for (size, peer, me), sums in zip(stages, (part, ysum, zsum)):
        sums[me] = mine
        copies = []
        for k in range(1, size):
            i, where = peer(k)
            copies.append(pltpu.make_async_remote_copy(
                src_ref=sums.at[me], dst_ref=sums.at[me],
                send_sem=nsend.at[base + k], recv_sem=nrecv.at[base + me],
                device_id=where, device_id_type=MESH,
            ))
        for copy in copies:
            copy.start()
        for k in range(1, size):
            i, where = peer(k)
            pltpu.make_async_remote_copy(
                src_ref=sums.at[i], dst_ref=sums.at[i],
                send_sem=nsend.at[base + k], recv_sem=nrecv.at[base + i],
                device_id=where, device_id_type=MESH,
            ).wait_recv()
        mine = sums[0]
        for i in range(1, size):
            mine = mine + sums[i]
        for copy in copies:
            copy.wait_send()
        base += size
    norm_ref[0, 0] = jnp.sqrt(jnp.sum(mine, axis=1, keepdims=True))[0, 0]

    for a in range(3):
        for group in app_copies(a):
            wait_send(group)
    wait_send(setup_copies())
    store.wait()


def solution(mesh):
    ny = mesh.shape["wf"] // PLANE
    members = ROW + ny + ZLO * PLANE

    def local(wavefunctions, cell_matrix, cell_nodes, home_counts, atom_start, projectors, coupling):
        hbm = pl.BlockSpec(memory_space=pl.ANY)
        vmem = pl.BlockSpec(memory_space=pltpu.VMEM)
        smem = pl.BlockSpec(memory_space=pltpu.SMEM)
        filtered, norm = pl.pallas_call(
            functools.partial(kernel, ny),
            out_shape=(
                jax.ShapeDtypeStruct((OWN, COLS), F32),
                jax.ShapeDtypeStruct((1, 1), F32),
            ),
            in_specs=[hbm, hbm, vmem, smem, smem, hbm, hbm],
            out_specs=(hbm, smem),
            scratch_shapes=[
                pltpu.VMEM((4, OWN, COLS), F32),
                pltpu.VMEM((3, OWN, COLS), BF16),
                pltpu.VMEM((3, GROWS, COLS), BF16),
                pltpu.VMEM((3, EXT, COLS), BF16),
                pltpu.VMEM((3, 2, BLK, COLS), BF16),
                pltpu.VMEM((3, 2, HOME, COLS), BF16),
                pltpu.VMEM((PROWS, COLS), F32),
                pltpu.VMEM((OWN, COLS), F32),
                pltpu.VMEM((CELLS, NPC, NPC), BF16),
                pltpu.VMEM((EXT, CELLS * NPC), BF16),
                pltpu.VMEM((EXT, CELLS * NPC), BF16),
                pltpu.VMEM((GROWS, OWN), BF16),
                pltpu.VMEM((OWN, OWN), BF16),
                pltpu.VMEM((OWN, OWN), BF16),
                pltpu.VMEM((OWN, EXT), BF16),
                pltpu.VMEM((2, GHOST, GHOST), F32),
                pltpu.VMEM((2, GHOST, 2 * GHOST), BF16),
                pltpu.VMEM((2, GHOST, 2 * GHOST), BF16),
                pltpu.VMEM((1, 3, ATOM_HOME, NPROJ, SUP), BF16),
                pltpu.VMEM((3 * ATOM_HOME * SLOT, OWN), F32),
                pltpu.VMEM((3 * ATOM_HOME * SLOT, OWN), BF16),
                pltpu.VMEM((ATOM_HOME, NPROJ, NPROJ), F32),
                pltpu.VMEM((ATOM_HOME * SLOT, 128), F32),
                pltpu.VMEM((ATOM_HOME * SLOT, 128), F32),
                pltpu.VMEM((2, ATOM_HOME * SLOT, 128), F32),
                pltpu.VMEM((3 * ATOM_HOME * SLOT, 256), F32),
                pltpu.VMEM((ROW, 1, COLS), F32),
                pltpu.VMEM((ny, 1, COLS), F32),
                pltpu.VMEM((ZLO * PLANE, 1, COLS), F32),
                pltpu.SemaphoreType.DMA((4,)),
                pltpu.SemaphoreType.DMA,
                pltpu.SemaphoreType.DMA((3, 8)),
                pltpu.SemaphoreType.DMA((3, 8)),
                pltpu.SemaphoreType.DMA((4,)),
                pltpu.SemaphoreType.DMA((4,)),
                pltpu.SemaphoreType.DMA((members,)),
                pltpu.SemaphoreType.DMA((members,)),
            ],
            compiler_params=pltpu.CompilerParams(collective_id=0, has_side_effects=True),
            name="chebyshev",
        )(wavefunctions, cell_matrix, cell_nodes, home_counts, atom_start, projectors, coupling)
        return filtered, norm.reshape(())

    return jax.shard_map(
        local,
        mesh=mesh,
        in_specs=(
            P("dom", "wf"),
            P("dom", None, None),
            P("dom", None),
            P("dom", None),
            P("dom", None, None),
            P("dom", None, None, None, None),
            P("dom", None, None),
        ),
        out_specs=(P("dom", "wf"), P()),
        check_vma=False,
    )
```

time: 348 us -> 62.2 us (0.18)
  blocking collectives: 135 us -> 0 us
  other arithmetic: 79.3 us -> 0 us
  starting transfers between devices: 72.9 us -> 0 us
  Pallas kernels: 0 us -> 53.4 us
  local copies, waits for them, and re-layouts: 46 us -> 5.89 us
  matrix products: 5.99 us -> 0 us
  waiting for transfers between devices: 4.73 us -> 0 us
    psum x1 -> x0, blocking collectives: 135 us -> none  [local(): block_total = lax.psum(jnp.sum(filtered * filtered), ('dom', 'wf'))]
    scatter-add x12 -> x0, other arithmetic: 74.4 us -> none  [the longest x3 52.3 us: apply_hamiltonian(): projected_part = jnp.zeros((own_rows, columns), jnp.float32).at[slot_rows...]
    ppermute x24 -> x0, starting transfers between devices: 72.9 us -> none  [the longest x12 41.6 us: with_halo(): before = lax.ppermute(last, axis, up)]
    pallas_call x0 -> x1, Pallas kernels: none -> 53.4 us  [local(): pl.pallas_call(functools.partial(kernel, ny), out_shape=(jax.ShapeDtypeSt...]
    gather x6 -> x0, local copies, waits for them, and re-layouts: 37.1 us -> none  [the longest x3 27.5 us: apply_hamiltonian(): windows = rounded[slot_rows]]
    dot_general x12 -> x0, matrix products: 5.99 us -> none  [the longest x3 3.24 us: apply_hamiltonian(): lax.dot_general(projector_flat, nearby, (((1,), (1,)), ((0,), (0,))), pre...]
    unnamed x43 -> x4, local copies, waits for them, and re-layouts: 0.13 us -> 5.89 us
    mul x3 -> x0, local copies, waits for them, and re-layouts: 4.95 us -> none  [apply_hamiltonian(): lax.dot_general(projector_flat, nearby, (((1,), (1,)), ((0,), (0,))), pre...]
  transfers between devices with their start and end apart: 24 -> 0, of which waited for: 4 -> 0; matrix products, arithmetic and copies ran while one was open for 12% -> 0% of each run, Pallas kernels for 0% -> 0%
where the time goes in v1:
time: 62.2 us; the launch traced here: 61.6 us
  Pallas kernels  53.4 us (86%)
  local copies, waits for them, and re-layouts  5.89 us (9%)
  between operations  2.33 us (4%)
    pallas_call x1, Pallas kernels, local(): pl.pallas_call(functools.partial(kernel, ny), out_shape=(jax.ShapeDtypeSt...  53.4 us
    unnamed x4, local copies, waits for them, and re-layouts  5.89 us

profile of v1, /device:TPU:1, one launch (start us, length us, event | category | flops | bytes accessed | tf_op | source)
XLA Modules:
  0.0 61.6 jit_solution(16145595970389719234)
XLA Ops:
  0.6 1.3 %copy.9.starts_ref = s32[1,3,4]{2,1,0:T(4,128)} copy(s32[1,3,4]{2,0,1:T(1,128)} %param.11) | data formatting | bytes 96 | tf_op args[4]
  1.9 1.4 %copy.11.coupling_ref = f32[4,18,18]{2,1,0:T(8,128)} copy(f32[4,18,18]{2,0,1:T(4,128)} %param.13) | data formatting | bytes 10368 | tf_op args[6]
  3.3 1.6 %copy.10.proj_ref = bf16[1,3,4,18,256]{4,3,2,1,0:T(8,128)(2,1)} copy(bf16[1,3,4,18,256]{4,2,3,1,0:T(4,128)(2,1)} %param.12) | data formatting | bytes 221184 | tf_op args[5]
  4.9 53.4 %chebyshev.1 = (f32[512,128]{1,0:T(8,128)}, f32[1,1]{1,0:T(1,128)}) custom-call(f32[512,128]{1,0:T(8,128)} %wave_ref.1, bf16[2,512,512]{2,1,0:T(8,128)(2,1)} %matrix_ref.1, s32[2,512]{1,0:T(2,128)} %nodes_ref.1, s32[1,3]{1,0:T(1,128)} %counts_ref.1, s32[1,3,4]{2,1,0:T(4,128)} %copy.9.starts_ref, bf16[1,3,4,18,256]{4,3,2,1,0:T(8,128)(2,1)} %copy.10.proj_ref, ...), custom_call_target="tpu_custom_call" | custom-call | tf_op jit(solution)/shard_map/chebyshev/pallas_call | solution.py:349
  58.2 1.7 %copy.14 = f32[512,128]{1,0:T(8,128)} copy(f32[512,128]{1,0:T(8,128)} %get-tuple-element.8) | data formatting | bytes 524288

commit v2 on v1

--- a/solution.py
+++ b/solution.py
@@ -47,7 +47,7 @@
     wave_ref, matrix_ref, nodes_ref, counts_ref, starts_ref, proj_ref, coupling_ref,
     out_ref, norm_ref,
     fv, vb, gb, xb, rblk, rc2, c32, acc,
-    cm, scat, tcat, gmat, ahi, alo, fmat, corner, csend, crecv,
+    cm, scat, tcat, gmat, amat, dtab, fmat, corner, csend, crecv,
     pin, pst, pall, cin, cst, csn, crc, call,
     part, ysum, zsum,
     in_sem, out_sem, send_sem, recv_sem, ssend_sem, srecv_sem,
@@ -63,25 +63,32 @@
         pltpu.make_async_copy(matrix_ref, cm, in_sem.at[2]),
         pltpu.make_async_copy(wave_ref, fv.at[0], in_sem.at[3]),
     ]
-    for load in loads:
-        load.start()
+    for i in (2, 0, 3, 1):
+        loads[i].start()
 
     zlo, row = lax.div(d, ROW), lax.rem(d, ROW)
     y, zhi = lax.div(w, PLANE), lax.rem(w, PLANE)
     z = zhi * ZLO + zlo
     nz = ZLO * PLANE
 
+    def around(i, size):
+        return i - size * (i >= size).astype(jnp.int32)
+
     def row_peer(k):
-        i = lax.rem(row + k, ROW)
+        i = around(row + k, ROW)
         return i, (zlo * ROW + i, w)
 
     def y_peer(k):
-        i = lax.rem(y + k, ny)
+        i = around(y + k, ny)
         return i, (d, i * PLANE + zhi)
 
     def z_peer(k):
-        i = lax.rem(z + k, nz)
-        return i, (lax.rem(i, ZLO) * ROW + row, y * PLANE + lax.div(i, ZLO))
+        i = around(z + k, nz)
+        hi = (i >= ZLO).astype(jnp.int32) + (i >= 2 * ZLO).astype(jnp.int32)
+        return i, ((i - ZLO * hi) * ROW + row, y * PLANE + hi)
+
+    def far_first(size):
+        return sorted(range(1, size), key=lambda k: -min(k, size - k))
 
     stages = ((ROW, row_peer, row), (ny, y_peer, y), (nz, z_peer, z))
 
@@ -91,7 +98,7 @@
         def _():
             pl.semaphore_signal(barrier, inc=1, device_id=(other, w), device_id_type=MESH)
     for size, peer, _ in stages:
-        for k in range(1, size):
+        for k in far_first(size):
             pl.semaphore_signal(barrier, inc=1, device_id=peer(k)[1], device_id_type=MESH)
 
     def zero(ref):
@@ -116,6 +123,7 @@
 
     for c in range(CELLS):
         nodes = nodes_ref[pl.ds(c, 1), :]
+        nodes = jnp.where(nodes < GHOST, nodes, jnp.where(nodes >= GHOST + OWN, nodes - OWN, nodes + GHOST))
         rows = lax.broadcasted_iota(jnp.int32, (EXT, NPC), 0)
         scat[:, c * NPC:(c + 1) * NPC] = jnp.where(rows == nodes, 1.0, 0.0).astype(BF16)
 
@@ -123,9 +131,9 @@
     for k in range(3):
         for j in range(ATOM_HOME):
             i = (k * ATOM_HOME + j) * SLOT
-            pst[pl.ds(i, NPROJ), pl.ds(0, SUP)] = pin[0, k, j].astype(F32)
+            pst[pl.ds(i, NPROJ), pl.ds(0, SUP)] = pin[0, k, :, j, :].astype(F32)
             live = jnp.where(j < counts_ref[0, k], 1.0, 0.0).astype(F32)
-            placed = pltpu.roll(pst[pl.ds(i, SLOT), :], starts_ref[0, k, j], axis=1)
+            placed = pltpu.roll(pst[pl.ds(i, SLOT), :], starts_ref[k, 0, j], axis=1)
             pst[pl.ds(i, SLOT), :] = placed * live
     pall[...] = pst[...].astype(BF16)
     col = lax.broadcasted_iota(jnp.int32, (1, 3 * ATOM_HOME * SLOT), 1)
@@ -139,24 +147,31 @@
 
     loads[1].wait()
     for j in range(ATOM_HOME):
-        cst[pl.ds(j * SLOT, NPROJ), pl.ds(0, NPROJ)] = cin[j]
+        cst[pl.ds(j * SLOT, NPROJ), pl.ds(0, NPROJ)] = cin[:, j, :]
         rows = cst[pl.ds(j * SLOT, SLOT), :]
         csn[pl.ds(j * SLOT, SLOT), :] = rows if j == 0 else pltpu.roll(rows, j * NPROJ, axis=1)
 
     loads[2].wait()
 
-    def assemble(start, rows):
+    rims = 2 * GHOST
+    eye = lax.broadcasted_iota(jnp.int32, (GHOST, GHOST), 0) == lax.broadcasted_iota(jnp.int32, (GHOST, GHOST), 1)
+
+    def place(rows):
         for c in range(CELLS):
-            tcat[pl.ds(start, rows), c * NPC:(c + 1) * NPC] = dot(
-                scat[pl.ds(start, rows), c * NPC:(c + 1) * NPC], cm[c]
-            ).astype(BF16)
-        return dot_nt(tcat[pl.ds(start, rows), :], scat[...])
-
-    for side, start, grow in ((0, 0, 0), (1, GHOST + OWN, LO)):
-        rim = assemble(start, GHOST)
-        gmat[pl.ds(grow, GHOST), :] = rim[:, GHOST:GHOST + OWN].astype(BF16)
-        csend[side, :, 0:GHOST] = rim[:, 0:GHOST].astype(BF16)
-        csend[side, :, GHOST:2 * GHOST] = rim[:, GHOST + OWN:].astype(BF16)
+            cell = pl.ds(c * NPC, NPC)
+            tcat[rows, cell] = dot(scat[rows, cell], cm[c]).astype(BF16)
+
+    place(pl.ds(0, rims))
+    rim = dot_nt(tcat[0:rims, :], scat[...])
+    gmat[pl.ds(0, GHOST), :] = rim[0:GHOST, rims:].astype(BF16)
+    gmat[pl.ds(LO, GHOST), :] = rim[GHOST:, rims:].astype(BF16)
+    for side in range(2):
+        ends = rim[side * GHOST:(side + 1) * GHOST, 0:rims]
+        rounded = ends.astype(BF16)
+        csend[side, 0:GHOST, :] = rounded
+        left = (ends - rounded.astype(F32))[:, side * GHOST:(side + 1) * GHOST]
+        left = jnp.sum(jnp.where(eye, left, 0.0), axis=0, keepdims=True)
+        csend[side, GHOST:, 0:GHOST] = jnp.broadcast_to(left, (16, GHOST)).astype(BF16)
 
     loads[3].wait()
     vb[0] = fv[0].astype(BF16)
@@ -231,28 +246,40 @@
         start(group)
     start(setup_copies())
 
-    def split(block, rows, cols):
-        high = block.astype(BF16)
-        ahi[rows, cols] = high
-        alo[rows, cols] = (block - high.astype(F32)).astype(BF16)
-
-    for q in range(4):
+    fmat[:, GHOST:3 * GHOST] = rim[:, rims:].T.astype(BF16)
+    place(pl.ds(rims, OWN))
+    first, second = pl.ds(rims, 256), pl.ds(rims + 256, 256)
+    cross = dot_nt(tcat[first, :], scat[second, :])
+    amat[0:256, 256:] = cross.astype(BF16)
+    amat[256:, 0:256] = cross.T.astype(BF16)
+
+    def diagonal(block, q):
+        rounded = block.astype(BF16)
         rows = pl.ds(q * GHOST, GHOST)
-        body = assemble((q + 1) * GHOST, GHOST)
-        split(body[:, GHOST:GHOST + OWN], rows, pl.ds(0, OWN))
-        if q == 0:
-            corner[0] = body[:, GHOST:2 * GHOST]
-        if q == 3:
-            corner[1] = body[:, OWN:OWN + GHOST]
-        fmat[rows, GHOST:2 * GHOST] = body[:, 0:GHOST].astype(BF16)
-        fmat[rows, 2 * GHOST:3 * GHOST] = body[:, GHOST + OWN:].astype(BF16)
+        amat[rows, rows] = rounded
+        left = jnp.sum(jnp.where(eye, block - rounded.astype(F32), 0.0), axis=1, keepdims=True)
+        dtab[rows, :] = jnp.broadcast_to(left, (GHOST, COLS))
+
+    for half, rows in ((0, first), (1, second)):
+        block = dot_nt(tcat[rows, :], scat[rows, :])
+        at = half * 256
+        amat[at:at + GHOST, at + GHOST:at + 256] = block[0:GHOST, GHOST:].astype(BF16)
+        amat[at + GHOST:at + 256, at:at + GHOST] = block[GHOST:, 0:GHOST].astype(BF16)
+        if half == 0:
+            corner[0] = block[0:GHOST, 0:GHOST]
+            diagonal(block[GHOST:, GHOST:], 1)
+        else:
+            diagonal(block[0:GHOST, 0:GHOST], 2)
+            corner[1] = block[GHOST:, GHOST:]
 
     wait_recv(setup_copies())
-    fmat[0:GHOST, 0:GHOST] = crecv[0, :, 0:GHOST]
-    fmat[OWN - GHOST:, 3 * GHOST:4 * GHOST] = crecv[1, :, GHOST:]
-    low, high = pl.ds(0, GHOST), pl.ds(OWN - GHOST, GHOST)
-    split(corner[0] + crecv[0, :, GHOST:].astype(F32), low, low)
-    split(corner[1] + crecv[1, :, 0:GHOST].astype(F32), high, high)
+    fmat[0:GHOST, 0:GHOST] = crecv[0, 0:GHOST, 0:GHOST]
+    fmat[OWN - GHOST:, 3 * GHOST:4 * GHOST] = crecv[1, 0:GHOST, GHOST:]
+    for side in range(2):
+        at = (1 - side) * GHOST
+        left = crecv[side, GHOST:, 0:GHOST].astype(F32)[0:1]
+        block = corner[side] + crecv[side, 0:GHOST, at:at + GHOST].astype(F32) + jnp.where(eye, left, 0.0)
+        diagonal(block, 3 * side)
     empty = jnp.zeros((ATOM_HOME * SLOT, 128), F32)
     for k, block in ((0, crc[0]), (1, csn[...]), (2, crc[1])):
         wide = jnp.concatenate([block, empty], axis=1)
@@ -277,8 +304,9 @@
             start(edges)
             project(a)
             start(blocks)
-        acc[...] = dot(ahi[...], vb[a]) + dot(alo[...], vb[a]) - centre * fv[a]
+        acc[...] = dot(amat[...], vb[a]) + (dtab[...] * vb[a].astype(F32) - centre * fv[a])
         wait_recv(edges)
+        acc[...] += dot(fmat[:, 0:OWN], xb[a, 0:OWN, :])
         wait_recv(blocks)
         below, above = rblk[a, 0].astype(F32), rblk[a, 1].astype(F32)
         own = c32[...]
@@ -291,7 +319,7 @@
         ).astype(BF16)
         acc[0:GHOST, :] += below[2 * HOME:]
         acc[OWN - GHOST:, :] += above[0:GHOST]
-        new = (acc[...] + dot(fmat[...], xb[a])) * scales[a]
+        new = (acc[...] + dot(fmat[:, OWN:], xb[a, OWN:, :])) * scales[a]
         if a > 0:
             new = new - backs[a] * fv[a - 1]
         fv[a + 1] = new
@@ -303,38 +331,40 @@
     store.start()
 
     mine = jnp.sum(fv[3] * fv[3], axis=0, keepdims=True)
-    base = 0
+    base, sent = 0, []
     for (size, peer, me), sums in zip(stages, (part, ysum, zsum)):
         sums[me] = mine
-        copies = []
-        for k in range(1, size):
-            i, where = peer(k)
-            copies.append(pltpu.make_async_remote_copy(
+        for k in far_first(size):
+            copy = pltpu.make_async_remote_copy(
                 src_ref=sums.at[me], dst_ref=sums.at[me],
                 send_sem=nsend.at[base + k], recv_sem=nrecv.at[base + me],
-                device_id=where, device_id_type=MESH,
-            ))
-        for copy in copies:
+                device_id=peer(k)[1], device_id_type=MESH,
+            )
             copy.start()
-        for k in range(1, size):
+            sent.append(copy)
+        if base == 0:
+            for a in range(3):
+                for group in app_copies(a):
+                    wait_send(group)
+            wait_send(setup_copies())
+        else:
+            for copy in sent:
+                copy.wait_send()
+            sent = []
+        for k in reversed(far_first(size)):
             i, where = peer(k)
             pltpu.make_async_remote_copy(
                 src_ref=sums.at[i], dst_ref=sums.at[i],
                 send_sem=nsend.at[base + k], recv_sem=nrecv.at[base + i],
                 device_id=where, device_id_type=MESH,
             ).wait_recv()
-        mine = sums[0]
-        for i in range(1, size):
-            mine = mine + sums[i]
-        for copy in copies:
-            copy.wait_send()
+        terms = [sums[i] for i in range(size)]
+        while len(terms) > 1:
+            terms = [sum(terms[i:i + 2][1:], terms[i]) for i in range(0, len(terms), 2)]
+        mine = terms[0]
         base += size
     norm_ref[0, 0] = jnp.sqrt(jnp.sum(mine, axis=1, keepdims=True))[0, 0]
 
-    for a in range(3):
-        for group in app_copies(a):
-            wait_send(group)
-    wait_send(setup_copies())
     store.wait()
 
 
@@ -368,15 +398,15 @@
                 pltpu.VMEM((EXT, CELLS * NPC), BF16),
                 pltpu.VMEM((GROWS, OWN), BF16),
                 pltpu.VMEM((OWN, OWN), BF16),
-                pltpu.VMEM((OWN, OWN), BF16),
+                pltpu.VMEM((OWN, COLS), F32),
                 pltpu.VMEM((OWN, EXT), BF16),
                 pltpu.VMEM((2, GHOST, GHOST), F32),
-                pltpu.VMEM((2, GHOST, 2 * GHOST), BF16),
-                pltpu.VMEM((2, GHOST, 2 * GHOST), BF16),
-                pltpu.VMEM((1, 3, ATOM_HOME, NPROJ, SUP), BF16),
+                pltpu.VMEM((2, GHOST + 16, 2 * GHOST), BF16),
+                pltpu.VMEM((2, GHOST + 16, 2 * GHOST), BF16),
+                pltpu.VMEM((1, 3, NPROJ, ATOM_HOME, SUP), BF16),
                 pltpu.VMEM((3 * ATOM_HOME * SLOT, OWN), F32),
                 pltpu.VMEM((3 * ATOM_HOME * SLOT, OWN), BF16),
-                pltpu.VMEM((ATOM_HOME, NPROJ, NPROJ), F32),
+                pltpu.VMEM((NPROJ, ATOM_HOME, NPROJ), F32),
                 pltpu.VMEM((ATOM_HOME * SLOT, 128), F32),
                 pltpu.VMEM((ATOM_HOME * SLOT, 128), F32),
                 pltpu.VMEM((2, ATOM_HOME * SLOT, 128), F32),
@@ -395,7 +425,10 @@
             ],
             compiler_params=pltpu.CompilerParams(collective_id=0, has_side_effects=True),
             name="chebyshev",
-        )(wavefunctions, cell_matrix, cell_nodes, home_counts, atom_start, projectors, coupling)
+        )(
+            wavefunctions, cell_matrix, cell_nodes, home_counts, atom_start.transpose(1, 0, 2),
+            projectors.transpose(0, 1, 3, 2, 4), coupling.transpose(1, 0, 2),
+        )
         return filtered, norm.reshape(())
 
     return jax.shard_map(

time: 62.2 us -> 57.5 us (0.924)
  local copies, waits for them, and re-layouts: 5.89 us -> 1.67 us
    unnamed x4 -> x1, local copies, waits for them, and re-layouts: 5.89 us -> 1.67 us
where the time goes in v2:
time: 57.5 us; the launch traced here: 56.9 us
  Pallas kernels  52.8 us (92%)
  between operations  2.41 us (4%)
  local copies, waits for them, and re-layouts  1.67 us (3%)
    pallas_call x1, Pallas kernels, local(): pl.pallas_call(functools.partial(kernel, ny), out_shape=(jax.ShapeDtypeSt...  52.8 us
    unnamed x1, local copies, waits for them, and re-layouts  1.67 us

profile of v2, /device:TPU:1, one launch (start us, length us, event | category | flops | bytes accessed | tf_op | source)
XLA Modules:
  0.0 56.9 jit_solution(13952924599468100092)
XLA Ops:
  0.6 52.8 %chebyshev.1 = (f32[512,128]{1,0:T(8,128)}, f32[1,1]{1,0:T(1,128)}) custom-call(f32[512,128]{1,0:T(8,128)} %wave_ref.1, bf16[2,512,512]{2,1,0:T(8,128)(2,1)} %matrix_ref.1, s32[2,512]{1,0:T(2,128)} %nodes_ref.1, s32[1,3]{1,0:T(1,128)} %counts_ref.1, s32[3,1,4]{2,1,0:T(1,128)} %bitcast.6, bf16[1,3,18,4,256]{4,3,2,1,0:T(4,128)(2,1)} %bitcast.4, ...), custom_call_target="tpu_custom_call" | custom-call | tf_op jit(solution)/shard_map/chebyshev/pallas_call | solution.py:379
  53.5 1.7 %copy.11 = f32[512,128]{1,0:T(8,128)} copy(f32[512,128]{1,0:T(8,128)} %get-tuple-element.8) | data formatting | bytes 524288

commit v3 on v2

v3 whole, which is shorter than its diff:
```python
import functools

import jax
import jax.numpy as jnp
from jax import lax
from jax.experimental import pallas as pl
from jax.experimental.pallas import tpu as pltpu
from jax.sharding import PartitionSpec as P

F32, BF16 = jnp.float32, jnp.bfloat16
MESH = pl.DeviceIdType.MESH

lower_edge = -1.0
cut_edge = 2.0
upper_edge = 9.0

CELLS = 2
NPC = 512
OWN = 512
GHOST = 128
EXT = OWN + 2 * GHOST
COLS = 128
NPROJ, SUP, ATOM_HOME = 18, 256, 4
SLOT = 24
HOME = 80
PROWS = 3 * HOME
GROWS = 2 * GHOST + PROWS
BLK = GHOST + 2 * HOME
LO = GHOST + PROWS
ROW, PLANE, ZLO = 8, 3, 4


def dot(a, b):
    return jnp.dot(a, b, preferred_element_type=F32)


def dot_nt(a, b):
    return lax.dot_general(a, b, (((1,), (1,)), ((), ())), preferred_element_type=F32)


def dot_tn(a, b):
    return lax.dot_general(a, b, (((0,), (0,)), ((), ())), preferred_element_type=F32)


def kernel(
    ny,
    wave_ref, matrix_ref, nodes_hbm, counts_hbm, starts_hbm, proj_ref, coupling_ref,
    out_ref, norm_ref,
    fv, vb, gb, xb, rblk, rc2, c32, acc,
    cm, scat, tcat, gmat, amat, dtab, fmat, corner, csend, crecv,
    nodes_ref, counts_ref, starts_ref, pin, pst, pall, cin, cst, csn, crc, call,
    part, zsum,
    in_sem, send_sem, recv_sem, ssend_sem, srecv_sem,
    nsend, nrecv,
):
    d, w = lax.axis_index("dom"), lax.axis_index("wf")
    n_dom = 32
    below1, below2, above1, above2 = d >= 1, d >= 2, d < n_dom - 1, d < n_dom - 2

    loads = [
        pltpu.make_async_copy(proj_ref, pin, in_sem.at[0]),
        pltpu.make_async_copy(coupling_ref, cin, in_sem.at[1]),
        pltpu.make_async_copy(matrix_ref, cm, in_sem.at[2]),
        pltpu.make_async_copy(wave_ref, fv.at[0], in_sem.at[3]),
        pltpu.make_async_copy(nodes_hbm, nodes_ref, in_sem.at[4]),
        pltpu.make_async_copy(counts_hbm, counts_ref, in_sem.at[5]),
        pltpu.make_async_copy(starts_hbm, starts_ref, in_sem.at[6]),
    ]
    for i in (4, 5, 6, 0, 3, 2, 1):
        loads[i].start()

    zlo, row = lax.div(d, ROW), lax.rem(d, ROW)
    y, zhi = lax.div(w, PLANE), lax.rem(w, PLANE)
    z = zhi * ZLO + zlo
    nz = ZLO * PLANE

    def around(i, size):
        return i - size * (i >= size).astype(jnp.int32)

    def far_first(peers):
        return [p[1:] for p in sorted(peers, key=lambda p: -p[0])]

    def short(k, size):
        return min(k, size - k)

    plane = []
    for j in range(ny):
        for k in range(ROW):
            if j or k:
                yj, rk = around(y + j, ny), around(row + k, ROW)
                plane.append((short(j, ny) + short(k, ROW) / 2, yj * ROW + rk, (zlo * ROW + rk, yj * PLANE + zhi)))
    column = []
    for k in range(1, nz):
        i = around(z + k, nz)
        hi = (i >= ZLO).astype(jnp.int32) + (i >= 2 * ZLO).astype(jnp.int32)
        column.append((short(k, nz), i, ((i - ZLO * hi) * ROW + row, y * PLANE + hi)))
    stages = ((far_first(plane), y * ROW + row), (far_first(column), z))

    barrier = pltpu.get_barrier_semaphore()
    for cond, other in ((below1, d - 1), (above1, d + 1), (below2, d - 2), (above2, d + 2)):
        @pl.when(cond)
        def _():
            pl.semaphore_signal(barrier, inc=1, device_id=(other, w), device_id_type=MESH)
    for peers, _ in stages:
        for _, where in peers:
            pl.semaphore_signal(barrier, inc=1, device_id=where, device_id_type=MESH)

    def zero(ref):
        ref[...] = jnp.zeros(ref.shape, ref.dtype)

    for a in range(3):
        zero(xb.at[a, pl.ds(OWN, EXT - OWN)])
    for cond, part1, part2 in ((below1, 0, 0), (above1, 1, 1)):
        @pl.when(jnp.logical_not(cond))
        def _():
            for a in range(3):
                zero(rblk.at[a, part1])
                zero(xb.at[a, pl.ds(part2 * GHOST, GHOST)])
            zero(crecv.at[part1])
            zero(crc.at[part1])
    for cond, part1, part2 in ((below2, 0, 2), (above2, 1, 3)):
        @pl.when(jnp.logical_not(cond))
        def _():
            for a in range(3):
                zero(rc2.at[a, part1])
                zero(xb.at[a, pl.ds(part2 * GHOST, GHOST)])
    zero(pst)
    zero(cst)

    loads[4].wait()
    for c in range(CELLS):
        nodes = nodes_ref[pl.ds(c, 1), :]
        nodes = jnp.where(nodes < GHOST, nodes, jnp.where(nodes >= GHOST + OWN, nodes - OWN, nodes + GHOST))
        rows = lax.broadcasted_iota(jnp.int32, (EXT, NPC), 0)
        scat[:, c * NPC:(c + 1) * NPC] = jnp.where(rows == nodes, 1.0, 0.0).astype(BF16)

    loads[5].wait()
    loads[6].wait()
    loads[0].wait()
    for k in range(3):
        for j in range(ATOM_HOME):
            i = (k * ATOM_HOME + j) * SLOT
            pst[pl.ds(i, NPROJ), pl.ds(0, SUP)] = pin[0, k, :, j, :].astype(F32)
            live = jnp.where(j < counts_ref[0, k], 1.0, 0.0).astype(F32)
            placed = pltpu.roll(pst[pl.ds(i, SLOT), :], starts_ref[k, 0, j], axis=1)
            pst[pl.ds(i, SLOT), :] = placed * live
    pall[...] = pst[...].astype(BF16)
    col = lax.broadcasted_iota(jnp.int32, (1, 3 * ATOM_HOME * SLOT), 1)
    slot, p = lax.div(col, SLOT), lax.rem(col, SLOT)
    target = lax.div(slot, ATOM_HOME) * HOME + lax.rem(slot, ATOM_HOME) * NPROJ + p
    target = jnp.where(p < NPROJ, target, -1)
    pick = jnp.where(
        lax.broadcasted_iota(jnp.int32, (PROWS, 3 * ATOM_HOME * SLOT), 0) == target, 1.0, 0.0
    ).astype(BF16)
    gmat[pl.ds(GHOST, PROWS), :] = dot(pick, pall[...]).astype(BF16)

    loads[1].wait()
    for j in range(ATOM_HOME):
        cst[pl.ds(j * SLOT, NPROJ), pl.ds(0, NPROJ)] = cin[:, j, :]
        rows = cst[pl.ds(j * SLOT, SLOT), :]
        csn[pl.ds(j * SLOT, SLOT), :] = rows if j == 0 else pltpu.roll(rows, j * NPROJ, axis=1)

    even = lax.rem(d, 2) == 0
    odd = jnp.logical_not(even)

    def both(*conds):
        return functools.reduce(jnp.logical_and, conds)

    def remote(src, dst, sems, other):
        return pltpu.make_async_remote_copy(
            src_ref=src, dst_ref=dst, send_sem=sems[0], recv_sem=sems[1],
            device_id=(other, w), device_id_type=MESH,
        )

    def app_copies(a):
        def sems(i, j=None):
            return send_sem.at[a, i if j is None else j], recv_sem.at[a, i]

        low, high = vb.at[a, pl.ds(0, GHOST)], vb.at[a, pl.ds(OWN - GHOST, GHOST)]

        def x(i):
            return xb.at[a, pl.ds(i * GHOST, GHOST)]

        def g(start, rows):
            return gb.at[a, pl.ds(start, rows)]

        near = [
            (above1, below1, high, x(0), sems(0), d + 1),
            (below1, above1, low, x(1), sems(1), d - 1),
        ]
        far = [
            (both(even, above2), below2, high, x(2), sems(2), d + 2),
            (both(odd, below2), above2, low, x(3), sems(3), d - 2),
        ]
        relay = [
            (both(even, below1), None, x(0), x(2), sems(2, 10), d + 1),
            (both(odd, above1), None, x(1), x(3), sems(3, 11), d - 1),
        ]
        coefs = [
            (above1, below1, g(GHOST + HOME, 2 * HOME), rblk.at[a, 0, pl.ds(0, 2 * HOME)], sems(4), d + 1),
            (below1, above1, g(GHOST, 2 * HOME), rblk.at[a, 1, pl.ds(GHOST, 2 * HOME)], sems(5), d - 1),
            (above2, below2, g(GHOST + 2 * HOME, HOME), rc2.at[a, 0], sems(6), d + 2),
            (below2, above2, g(GHOST, HOME), rc2.at[a, 1], sems(7), d - 2),
        ]
        rim_sums = [
            (above1, below1, g(LO, GHOST), rblk.at[a, 0, pl.ds(2 * HOME, GHOST)], sems(8), d + 1),
            (below1, above1, g(0, GHOST), rblk.at[a, 1, pl.ds(0, GHOST)], sems(9), d - 1),
        ]
        return near, far, relay, coefs, rim_sums

    def setup_copies():
        def sems(i):
            return ssend_sem.at[i], srecv_sem.at[i]

        corners = [
            (above1, below1, csend.at[1], crecv.at[0], sems(0), d + 1),
            (below1, above1, csend.at[0], crecv.at[1], sems(1), d - 1),
        ]
        couplings = [
            (above1, below1, csn, crc.at[0], sems(2), d + 1),
            (below1, above1, csn, crc.at[1], sems(3), d - 1),
        ]
        return corners, couplings

    def start(copies):
        for cond, _, src, dst, sems, other in copies:
            @pl.when(cond)
            def _():
                remote(src, dst, sems, other).start()

    def wait_recv(copies):
        for _, cond, src, dst, sems, other in copies:
            @pl.when(cond)
            def _():
                remote(src, dst, sems, other).wait_recv()

    def wait_send(copies):
        for cond, _, src, dst, sems, other in copies:
            @pl.when(cond)
            def _():
                remote(src, dst, sems, other).wait_send()

    def project(a):
        coefs = dot(gmat[GHOST:LO, :], vb[a])
        gb[a, GHOST:LO, :] = coefs.astype(BF16)
        c32[...] = coefs

    def sum_rims(a):
        gb[a, 0:GHOST, :] = dot(gmat[0:GHOST, :], vb[a]).astype(BF16)
        gb[a, LO:, :] = dot(gmat[LO:, :], vb[a]).astype(BF16)

    loads[3].wait()
    vb[0] = fv[0].astype(BF16)
    project(0)
    pl.semaphore_wait(
        barrier,
        sum(len(peers) for peers, _ in stages) + below1.astype(jnp.int32) + below2.astype(jnp.int32)
        + above1.astype(jnp.int32) + above2.astype(jnp.int32),
    )
    for i in (0, 1, 3):
        start(app_copies(0)[i])
    start(setup_copies()[1])

    loads[2].wait()

    rims = 2 * GHOST
    eye = lax.broadcasted_iota(jnp.int32, (GHOST, GHOST), 0) == lax.broadcasted_iota(jnp.int32, (GHOST, GHOST), 1)

    def place(rows):
        for c in range(CELLS):
            cell = pl.ds(c * NPC, NPC)
            tcat[rows, cell] = dot(scat[rows, cell], cm[c]).astype(BF16)

    place(pl.ds(0, rims))
    rim = dot_nt(tcat[0:rims, :], scat[...])
    gmat[pl.ds(0, GHOST), :] = rim[0:GHOST, rims:].astype(BF16)
    gmat[pl.ds(LO, GHOST), :] = rim[GHOST:, rims:].astype(BF16)
    for side in range(2):
        ends = rim[side * GHOST:(side + 1) * GHOST, 0:rims]
        rounded = ends.astype(BF16)
        csend[side, 0:GHOST, :] = rounded
        left = (ends - rounded.astype(F32))[:, side * GHOST:(side + 1) * GHOST]
        left = jnp.sum(jnp.where(eye, left, 0.0), axis=0, keepdims=True)
        csend[side, GHOST:, 0:GHOST] = jnp.broadcast_to(left, (16, GHOST)).astype(BF16)

    near, far, relay, coefs, rim_sums = app_copies(0)
    corners, couplings = setup_copies()
    sum_rims(0)
    start(rim_sums)
    start(corners)
    wait_recv(near)
    start(relay)

    fmat[:, 0:rims] = rim[:, rims:].T.astype(BF16)
    place(pl.ds(rims, OWN))
    first, second = pl.ds(rims, 256), pl.ds(rims + 256, 256)
    cross = dot_nt(tcat[first, :], scat[second, :])
    amat[0:256, 256:] = cross.astype(BF16)
    amat[256:, 0:256] = cross.T.astype(BF16)

    def diagonal(block, q):
        rounded = block.astype(BF16)
        rows = pl.ds(q * GHOST, GHOST)
        amat[rows, rows] = rounded
        left = jnp.sum(jnp.where(eye, block - rounded.astype(F32), 0.0), axis=1, keepdims=True)
        dtab[rows, :] = jnp.broadcast_to(left, (GHOST, COLS))

    for half, rows in ((0, first), (1, second)):
        block = dot_nt(tcat[rows, :], scat[rows, :])
        at = half * 256
        amat[at:at + GHOST, at + GHOST:at + 256] = block[0:GHOST, GHOST:].astype(BF16)
        amat[at + GHOST:at + 256, at:at + GHOST] = block[GHOST:, 0:GHOST].astype(BF16)
        if half == 0:
            corner[0] = block[0:GHOST, 0:GHOST]
            diagonal(block[GHOST:, GHOST:], 1)
        else:
            diagonal(block[0:GHOST, 0:GHOST], 2)
            corner[1] = block[GHOST:, GHOST:]

    wait_recv(couplings)
    wait_recv(corners)
    for side in range(2):
        at = (1 - side) * GHOST
        left = crecv[side, GHOST:, 0:GHOST].astype(F32)[0:1]
        block = corner[side] + crecv[side, 0:GHOST, at:at + GHOST].astype(F32) + jnp.where(eye, left, 0.0)
        diagonal(block, 3 * side)
    empty = jnp.zeros((ATOM_HOME * SLOT, 128), F32)
    for k, block in ((0, crc[0]), (1, csn[...]), (2, crc[1])):
        wide = jnp.concatenate([block, empty], axis=1)
        call[pl.ds(k * ATOM_HOME * SLOT, ATOM_HOME * SLOT), :] = wide if k == 0 else pltpu.roll(wide, k * HOME, axis=1)
    couple = call[...]
    couple_hi = couple.astype(BF16)
    couple_lo = (couple - couple_hi.astype(F32)).astype(BF16)
    fmat[:, rims:] = (dot_tn(pall[...], couple_hi) + dot_tn(pall[...], couple_lo)).astype(BF16)

    half_width = (upper_edge - cut_edge) / 2.0
    centre = (upper_edge + cut_edge) / 2.0
    sigma_one = half_width / (lower_edge - centre)
    gamma_ratio = 2.0 / sigma_one
    sigma_two = 1.0 / (gamma_ratio - sigma_one)
    sigma_three = 1.0 / (gamma_ratio - sigma_two)
    scales = (sigma_one / half_width, 2.0 * sigma_two / half_width, 2.0 * sigma_three / half_width)
    backs = (0.0, sigma_one * sigma_two, sigma_two * sigma_three)

    for a in range(3):
        near, far, relay, coefs, rim_sums = app_copies(a)
        if a > 0:
            start(near)
            start(far)
            project(a)
            start(coefs)
            sum_rims(a)
            start(rim_sums)
        acc[...] = dot(amat[...], vb[a]) + (dtab[...] * vb[a].astype(F32) - centre * fv[a])
        if a > 0:
            wait_recv(near)
            start(relay)
        acc[...] += dot(fmat[:, 0:rims], xb[a, 0:rims, :])
        wait_recv(coefs)
        below, above = rblk[a, 0, 0:2 * HOME, :].astype(F32), rblk[a, 1, GHOST:, :].astype(F32)
        own = c32[...]
        xb[a, OWN:OWN + HOME, :] = (own[0:HOME] + below[0:HOME] + rc2[a, 0].astype(F32)).astype(BF16)
        xb[a, OWN + HOME:OWN + 2 * HOME, :] = (
            own[HOME:2 * HOME] + below[HOME:2 * HOME] + above[0:HOME]
        ).astype(BF16)
        xb[a, OWN + 2 * HOME:OWN + 3 * HOME, :] = (
            own[2 * HOME:] + above[HOME:] + rc2[a, 1].astype(F32)
        ).astype(BF16)
        acc[...] += dot(fmat[:, rims:], xb[a, OWN:, :])
        wait_recv(far)
        wait_recv(rim_sums)
        acc[0:GHOST, :] += rblk[a, 0, 2 * HOME:, :].astype(F32) + dot(
            crecv[0, 0:GHOST, 0:GHOST], xb[a, 2 * GHOST:3 * GHOST, :]
        )
        acc[OWN - GHOST:, :] += rblk[a, 1, 0:GHOST, :].astype(F32) + dot(
            crecv[1, 0:GHOST, GHOST:], xb[a, 3 * GHOST:4 * GHOST, :]
        )
        new = acc[...] * scales[a]
        if a > 0:
            new = new - backs[a] * fv[a - 1]
        if a == 2:
            out_ref[...] = new
        else:
            fv[a + 1] = new
            vb[a + 1] = new.astype(BF16)

    mine = jnp.sum(new * new, axis=0, keepdims=True)
    base, sent = 0, []
    for (peers, me), sums in zip(stages, (part, zsum)):
        sums[me] = mine
        for k, (_, where) in enumerate(peers):
            copy = pltpu.make_async_remote_copy(
                src_ref=sums.at[me], dst_ref=sums.at[me],
                send_sem=nsend.at[base + k], recv_sem=nrecv.at[base + me],
                device_id=where, device_id_type=MESH,
            )
            copy.start()
            sent.append(copy)
        if base == 0:
            for a in range(3):
                for group in app_copies(a):
                    wait_send(group)
            for group in setup_copies():
                wait_send(group)
        else:
            for copy in sent:
                copy.wait_send()
        for k, (i, where) in reversed(list(enumerate(peers))):
            pltpu.make_async_remote_copy(
                src_ref=sums.at[i], dst_ref=sums.at[i],
                send_sem=nsend.at[base + k], recv_sem=nrecv.at[base + i],
                device_id=where, device_id_type=MESH,
            ).wait_recv()
        size = len(peers) + 1
        terms = [sums[i] for i in range(size)]
        while len(terms) > 1:
            terms = [sum(terms[i:i + 2][1:], terms[i]) for i in range(0, len(terms), 2)]
        mine = terms[0]
        base += size
    norm_ref[0, 0] = jnp.sqrt(jnp.sum(mine, axis=1, keepdims=True))[0, 0]


def solution(mesh):
    ny = mesh.shape["wf"] // PLANE
    members = ROW * ny + ZLO * PLANE

    def local(wavefunctions, cell_matrix, cell_nodes, home_counts, atom_start, projectors, coupling):
        hbm = pl.BlockSpec(memory_space=pl.ANY)
        vmem = pl.BlockSpec(memory_space=pltpu.VMEM)
        smem = pl.BlockSpec(memory_space=pltpu.SMEM)
        filtered, norm = pl.pallas_call(
            functools.partial(kernel, ny),
            out_shape=(
                pltpu.VMEM((OWN, COLS), F32),
                jax.ShapeDtypeStruct((1, 1), F32),
            ),
            in_specs=[hbm] * 7,
            out_specs=(vmem, smem),
            scratch_shapes=[
                pltpu.VMEM((4, OWN, COLS), F32),
                pltpu.VMEM((3, OWN, COLS), BF16),
                pltpu.VMEM((3, GROWS, COLS), BF16),
                pltpu.VMEM((3, EXT, COLS), BF16),
                pltpu.VMEM((3, 2, BLK, COLS), BF16),
                pltpu.VMEM((3, 2, HOME, COLS), BF16),
                pltpu.VMEM((PROWS, COLS), F32),
                pltpu.VMEM((OWN, COLS), F32),
                pltpu.VMEM((CELLS, NPC, NPC), BF16),
                pltpu.VMEM((EXT, CELLS * NPC), BF16),
                pltpu.VMEM((EXT, CELLS * NPC), BF16),
                pltpu.VMEM((GROWS, OWN), BF16),
                pltpu.VMEM((OWN, OWN), BF16),
                pltpu.VMEM((OWN, COLS), F32),
                pltpu.VMEM((OWN, 2 * GHOST + 256), BF16),
                pltpu.VMEM((2, GHOST, GHOST), F32),
                pltpu.VMEM((2, GHOST + 16, 2 * GHOST), BF16),
                pltpu.VMEM((2, GHOST + 16, 2 * GHOST), BF16),
                pltpu.VMEM((CELLS, NPC), jnp.int32),
                pltpu.SMEM((1, 3), jnp.int32),
                pltpu.SMEM((3, 1, ATOM_HOME), jnp.int32),
                pltpu.VMEM((1, 3, NPROJ, ATOM_HOME, SUP), BF16),
                pltpu.VMEM((3 * ATOM_HOME * SLOT, OWN), F32),
                pltpu.VMEM((3 * ATOM_HOME * SLOT, OWN), BF16),
                pltpu.VMEM((NPROJ, ATOM_HOME, NPROJ), F32),
                pltpu.VMEM((ATOM_HOME * SLOT, 128), F32),
                pltpu.VMEM((ATOM_HOME * SLOT, 128), F32),
                pltpu.VMEM((2, ATOM_HOME * SLOT, 128), F32),
                pltpu.VMEM((3 * ATOM_HOME * SLOT, 256), F32),
                pltpu.VMEM((ROW * ny, 1, COLS), F32),
                pltpu.VMEM((ZLO * PLANE, 1, COLS), F32),
                pltpu.SemaphoreType.DMA((7,)),
                pltpu.SemaphoreType.DMA((3, 12)),
                pltpu.SemaphoreType.DMA((3, 10)),
                pltpu.SemaphoreType.DMA((4,)),
                pltpu.SemaphoreType.DMA((4,)),
                pltpu.SemaphoreType.DMA((members,)),
                pltpu.SemaphoreType.DMA((members,)),
            ],
            compiler_params=pltpu.CompilerParams(collective_id=0, has_side_effects=True),
            name="chebyshev",
        )(
            wavefunctions, cell_matrix, cell_nodes, home_counts, atom_start.transpose(1, 0, 2),
            projectors.transpose(0, 1, 3, 2, 4), coupling.transpose(1, 0, 2),
        )
        return filtered, norm.reshape(())

    return jax.shard_map(
        local,
        mesh=mesh,
        in_specs=(
            P("dom", "wf"),
            P("dom", None, None),
            P("dom", None),
            P("dom", None),
            P("dom", None, None),
            P("dom", None, None, None, None),
            P("dom", None, None),
        ),
        out_specs=(P("dom", "wf"), P()),
        check_vma=False,
    )
```

time: 57.5 us -> 54 us (0.939)
  Pallas kernels: 52.8 us -> 50.9 us
  local copies, waits for them, and re-layouts: 1.67 us -> 0.71 us
    pallas_call x1, Pallas kernels: 52.8 us -> 50.9 us  [local(): pl.pallas_call(functools.partial(kernel, ny), out_shape=(pltpu.VMEM((OWN,...]
    unnamed x1, local copies, waits for them, and re-layouts: 1.67 us -> 0.71 us
where the time goes in v3:
time: 54 us; the launch traced here: 53.9 us
  Pallas kernels  50.9 us (94%)
  between operations  2.33 us (4%)
  local copies, waits for them, and re-layouts  0.71 us (1%)
    pallas_call x1, Pallas kernels, local(): pl.pallas_call(functools.partial(kernel, ny), out_shape=(pltpu.VMEM((OWN,...  50.9 us

profile of v3, /device:TPU:1, one launch (start us, length us, event | category | flops | bytes accessed | tf_op | source)
XLA Modules:
  0.0 53.9 jit_solution(6110910255894172201)
XLA Ops:
  0.6 50.9 %chebyshev.1 = (f32[512,128]{1,0:T(8,128)S(1)}, f32[1,1]{1,0:T(1,128)}) custom-call(f32[512,128]{1,0:T(8,128)} %wave_ref.1, bf16[2,512,512]{2,1,0:T(8,128)(2,1)} %matrix_ref.1, s32[2,512]{1,0:T(2,128)} %nodes_hbm.1, s32[1,3]{1,0:T(1,128)} %counts_hbm.1, s32[3,1,4]{2,1,0:T(1,128)} %bitcast.6, bf16[1,3,18,4,256]{4,3,2,1,0:T(4,128)(2,1)} %bitcast.4, ...), custom_call_target="tpu_custom_call" | custom-call | tf_op jit(solution)/shard_map/chebyshev/pallas_call | solution.py:431
  51.5 0.7 %copy.11 = f32[512,128]{1,0:T(8,128)} copy(f32[512,128]{1,0:T(8,128)S(1)} %get-tuple-element.6) | data formatting | bytes 524288

commit v4 on v3

--- a/solution.py
+++ b/solution.py
@@ -51,7 +51,7 @@
     nodes_ref, counts_ref, starts_ref, pin, pst, pall, cin, cst, csn, crc, call,
     part, zsum,
     in_sem, send_sem, recv_sem, ssend_sem, srecv_sem,
-    nsend, nrecv,
+    nsend, nrecv, token,
 ):
     d, w = lax.axis_index("dom"), lax.axis_index("wf")
     n_dom = 32
@@ -96,14 +96,34 @@
         column.append((short(k, nz), i, ((i - ZLO * hi) * ROW + row, y * PLANE + hi)))
     stages = ((far_first(plane), y * ROW + row), (far_first(column), z))
 
+    def ring(dy, dz):
+        j, i = around(y + dy % ny, ny), around(z + dz % nz, nz)
+        hi = (i >= ZLO).astype(jnp.int32) + (i >= 2 * ZLO).astype(jnp.int32)
+        return (i - ZLO * hi) * ROW + row, j * PLANE + hi
+
+    beside = [(zlo * ROW + around(row + k, ROW), w) for k in range(1, ROW)]
+    next_ones = [ring(1, 0), ring(-1, 0), ring(0, 1), ring(0, -1)]
+    beside = beside + next_ones
+    tokens = [
+        next_ones,
+        [ring(2, 0), ring(-2, 0), ring(0, 2), ring(0, -2)],
+        [ring(1, 0), ring(-1, 0), ring(0, 2), ring(0, -2)],
+    ]
+
+    def send_token(i):
+        for where in tokens[i]:
+            pl.semaphore_signal(token.at[i], inc=1, device_id=where, device_id_type=MESH)
+
+    def wait_token(i):
+        pl.semaphore_wait(token.at[i], len(tokens[i]))
+
     barrier = pltpu.get_barrier_semaphore()
     for cond, other in ((below1, d - 1), (above1, d + 1), (below2, d - 2), (above2, d + 2)):
         @pl.when(cond)
         def _():
             pl.semaphore_signal(barrier, inc=1, device_id=(other, w), device_id_type=MESH)
-    for peers, _ in stages:
-        for _, where in peers:
-            pl.semaphore_signal(barrier, inc=1, device_id=where, device_id_type=MESH)
+    for where in beside:
+        pl.semaphore_signal(barrier, inc=1, device_id=where, device_id_type=MESH)
 
     def zero(ref):
         ref[...] = jnp.zeros(ref.shape, ref.dtype)
@@ -254,12 +274,13 @@
     project(0)
     pl.semaphore_wait(
         barrier,
-        sum(len(peers) for peers, _ in stages) + below1.astype(jnp.int32) + below2.astype(jnp.int32)
+        len(beside) + below1.astype(jnp.int32) + below2.astype(jnp.int32)
         + above1.astype(jnp.int32) + above2.astype(jnp.int32),
     )
     for i in (0, 1, 3):
         start(app_copies(0)[i])
     start(setup_copies()[1])
+    send_token(0)
 
     loads[2].wait()
 
@@ -319,6 +340,8 @@
 
     wait_recv(couplings)
     wait_recv(corners)
+    wait_token(0)
+    send_token(1)
     for side in range(2):
         at = (1 - side) * GHOST
         left = crecv[side, GHOST:, 0:GHOST].astype(F32)[0:1]
@@ -351,6 +374,9 @@
             start(coefs)
             sum_rims(a)
             start(rim_sums)
+            wait_token(a)
+            if a == 1:
+                send_token(2)
         acc[...] = dot(amat[...], vb[a]) + (dtab[...] * vb[a].astype(F32) - centre * fv[a])
         if a > 0:
             wait_recv(near)
@@ -475,6 +501,7 @@
                 pltpu.SemaphoreType.DMA((4,)),
                 pltpu.SemaphoreType.DMA((members,)),
                 pltpu.SemaphoreType.DMA((members,)),
+                pltpu.SemaphoreType.REGULAR((3,)),
             ],
             compiler_params=pltpu.CompilerParams(collective_id=0, has_side_effects=True),
             name="chebyshev",

time: 54 us -> 51.2 us (0.948)
  Pallas kernels: 50.9 us -> 48 us
    pallas_call x1, Pallas kernels: 50.9 us -> 48 us  [local(): pl.pallas_call(functools.partial(kernel, ny), out_shape=(pltpu.VMEM((OWN,...]
where the time goes in v4:
time: 51.2 us; the launch traced here: 51 us
  Pallas kernels  48 us (94%)
  between operations  2.33 us (5%)
  local copies, waits for them, and re-layouts  0.71 us (1%)
    pallas_call x1, Pallas kernels, local(): pl.pallas_call(functools.partial(kernel, ny), out_shape=(pltpu.VMEM((OWN,...  48 us

profile of v4, /device:TPU:1, one launch (start us, length us, event | category | flops | bytes accessed | tf_op | source)
XLA Modules:
  0.0 51.0 jit_solution(4086992388526080486)
XLA Ops:
  0.6 48.0 %chebyshev.1 = (f32[512,128]{1,0:T(8,128)S(1)}, f32[1,1]{1,0:T(1,128)}) custom-call(f32[512,128]{1,0:T(8,128)} %wave_ref.1, bf16[2,512,512]{2,1,0:T(8,128)(2,1)} %matrix_ref.1, s32[2,512]{1,0:T(2,128)} %nodes_hbm.1, s32[1,3]{1,0:T(1,128)} %counts_hbm.1, s32[3,1,4]{2,1,0:T(1,128)} %bitcast.6, bf16[1,3,18,4,256]{4,3,2,1,0:T(4,128)(2,1)} %bitcast.4, ...), custom_call_target="tpu_custom_call" | custom-call | tf_op jit(solution)/shard_map/chebyshev/pallas_call | solution.py:457
  48.6 0.7 %copy.11 = f32[512,128]{1,0:T(8,128)} copy(f32[512,128]{1,0:T(8,128)S(1)} %get-tuple-element.6) | data formatting | bytes 524288

commit v5 on v4

--- a/solution.py
+++ b/solution.py
@@ -22,7 +22,7 @@
 COLS = 128
 NPROJ, SUP, ATOM_HOME = 18, 256, 4
 SLOT = 24
-HOME = 80
+HOME = 72
 PROWS = 3 * HOME
 GROWS = 2 * GHOST + PROWS
 BLK = GHOST + 2 * HOME
@@ -138,11 +138,17 @@
                 zero(xb.at[a, pl.ds(part2 * GHOST, GHOST)])
             zero(crecv.at[part1])
             zero(crc.at[part1])
-    for cond, part1, part2 in ((below2, 0, 2), (above2, 1, 3)):
+    even = lax.rem(d, 2) == 0
+    odd = jnp.logical_not(even)
+    for cond, passed, part1, part2 in ((below2, odd, 0, 2), (above2, even, 1, 3)):
         @pl.when(jnp.logical_not(cond))
         def _():
             for a in range(3):
                 zero(rc2.at[a, part1])
+
+        @pl.when(jnp.logical_not(jnp.logical_and(cond, passed)))
+        def _():
+            for a in range(3):
                 zero(xb.at[a, pl.ds(part2 * GHOST, GHOST)])
     zero(pst)
     zero(cst)
@@ -180,9 +186,6 @@
         rows = cst[pl.ds(j * SLOT, SLOT), :]
         csn[pl.ds(j * SLOT, SLOT), :] = rows if j == 0 else pltpu.roll(rows, j * NPROJ, axis=1)
 
-    even = lax.rem(d, 2) == 0
-    odd = jnp.logical_not(even)
-
     def both(*conds):
         return functools.reduce(jnp.logical_and, conds)
 
@@ -208,13 +211,9 @@
             (above1, below1, high, x(0), sems(0), d + 1),
             (below1, above1, low, x(1), sems(1), d - 1),
         ]
-        far = [
-            (both(even, above2), below2, high, x(2), sems(2), d + 2),
-            (both(odd, below2), above2, low, x(3), sems(3), d - 2),
-        ]
         relay = [
-            (both(even, below1), None, x(0), x(2), sems(2, 10), d + 1),
-            (both(odd, above1), None, x(1), x(3), sems(3, 11), d - 1),
+            (both(even, below1), both(odd, below2), x(0), x(2), sems(2, 10), d + 1),
+            (both(odd, above1), both(even, above2), x(1), x(3), sems(3, 11), d - 1),
         ]
         coefs = [
             (above1, below1, g(GHOST + HOME, 2 * HOME), rblk.at[a, 0, pl.ds(0, 2 * HOME)], sems(4), d + 1),
@@ -226,7 +225,7 @@
             (above1, below1, g(LO, GHOST), rblk.at[a, 0, pl.ds(2 * HOME, GHOST)], sems(8), d + 1),
             (below1, above1, g(0, GHOST), rblk.at[a, 1, pl.ds(0, GHOST)], sems(9), d - 1),
         ]
-        return near, far, relay, coefs, rim_sums
+        return near, relay, coefs, rim_sums
 
     def setup_copies():
         def sems(i):
@@ -265,9 +264,29 @@
         gb[a, GHOST:LO, :] = coefs.astype(BF16)
         c32[...] = coefs
 
-    def sum_rims(a):
-        gb[a, 0:GHOST, :] = dot(gmat[0:GHOST, :], vb[a]).astype(BF16)
-        gb[a, LO:, :] = dot(gmat[LO:, :], vb[a]).astype(BF16)
+    def sum_rims(a, near):
+        low, high = dot(gmat[0:GHOST, :], vb[a]), dot(gmat[LO:, :], vb[a])
+
+        @pl.when(odd)
+        def _():
+            wait_recv(near[0:1])
+            gb[a, 0:GHOST, :] = low.astype(BF16)
+            gb[a, LO:, :] = (high + dot(csend[1, 0:GHOST, 0:GHOST], xb[a, 0:GHOST, :])).astype(BF16)
+
+        @pl.when(even)
+        def _():
+            wait_recv(near[1:2])
+            gb[a, 0:GHOST, :] = (low + dot(csend[0, 0:GHOST, GHOST:], xb[a, GHOST:2 * GHOST, :])).astype(BF16)
+            gb[a, LO:, :] = high.astype(BF16)
+
+    def wait_linked(near):
+        @pl.when(odd)
+        def _():
+            wait_recv(near[1:2])
+
+        @pl.when(even)
+        def _():
+            wait_recv(near[0:1])
 
     loads[3].wait()
     vb[0] = fv[0].astype(BF16)
@@ -277,7 +296,7 @@
         len(beside) + below1.astype(jnp.int32) + below2.astype(jnp.int32)
         + above1.astype(jnp.int32) + above2.astype(jnp.int32),
     )
-    for i in (0, 1, 3):
+    for i in (0, 2):
         start(app_copies(0)[i])
     start(setup_copies()[1])
     send_token(0)
@@ -304,12 +323,12 @@
         left = jnp.sum(jnp.where(eye, left, 0.0), axis=0, keepdims=True)
         csend[side, GHOST:, 0:GHOST] = jnp.broadcast_to(left, (16, GHOST)).astype(BF16)
 
-    near, far, relay, coefs, rim_sums = app_copies(0)
+    near, relay, coefs, rim_sums = app_copies(0)
     corners, couplings = setup_copies()
-    sum_rims(0)
+    sum_rims(0, near)
     start(rim_sums)
     start(corners)
-    wait_recv(near)
+    wait_linked(near)
     start(relay)
 
     fmat[:, 0:rims] = rim[:, rims:].T.astype(BF16)
@@ -366,20 +385,19 @@
     backs = (0.0, sigma_one * sigma_two, sigma_two * sigma_three)
 
     for a in range(3):
-        near, far, relay, coefs, rim_sums = app_copies(a)
+        near, relay, coefs, rim_sums = app_copies(a)
         if a > 0:
             start(near)
-            start(far)
             project(a)
             start(coefs)
-            sum_rims(a)
+            sum_rims(a, near)
             start(rim_sums)
             wait_token(a)
             if a == 1:
                 send_token(2)
         acc[...] = dot(amat[...], vb[a]) + (dtab[...] * vb[a].astype(F32) - centre * fv[a])
         if a > 0:
-            wait_recv(near)
+            wait_linked(near)
             start(relay)
         acc[...] += dot(fmat[:, 0:rims], xb[a, 0:rims, :])
         wait_recv(coefs)
@@ -393,7 +411,7 @@
             own[2 * HOME:] + above[HOME:] + rc2[a, 1].astype(F32)
         ).astype(BF16)
         acc[...] += dot(fmat[:, rims:], xb[a, OWN:, :])
-        wait_recv(far)
+        wait_recv(relay)
         wait_recv(rim_sums)
         acc[0:GHOST, :] += rblk[a, 0, 2 * HOME:, :].astype(F32) + dot(
             crecv[0, 0:GHOST, 0:GHOST], xb[a, 2 * GHOST:3 * GHOST, :]

time: 51.2 us -> 50.9 us (level)
  no operation moved by 1% of the time
where the time goes in v5:
time: 50.9 us; the launch traced here: 50.7 us
  Pallas kernels  47.7 us (94%)
  between operations  2.33 us (5%)
  local copies, waits for them, and re-layouts  0.71 us (1%)
    pallas_call x1, Pallas kernels, local(): pl.pallas_call(functools.partial(kernel, ny), out_shape=(pltpu.VMEM((OWN,...  47.7 us

profile of v5, /device:TPU:1, one launch (start us, length us, event | category | flops | bytes accessed | tf_op | source)
XLA Modules:
  0.0 50.7 jit_solution(3335644531151187805)
XLA Ops:
  0.6 47.7 %chebyshev.1 = (f32[512,128]{1,0:T(8,128)S(1)}, f32[1,1]{1,0:T(1,128)}) custom-call(f32[512,128]{1,0:T(8,128)} %wave_ref.1, bf16[2,512,512]{2,1,0:T(8,128)(2,1)} %matrix_ref.1, s32[2,512]{1,0:T(2,128)} %nodes_hbm.1, s32[1,3]{1,0:T(1,128)} %counts_hbm.1, s32[3,1,4]{2,1,0:T(1,128)} %bitcast.6, bf16[1,3,18,4,256]{4,3,2,1,0:T(4,128)(2,1)} %bitcast.4, ...), custom_call_target="tpu_custom_call" | custom-call | tf_op jit(solution)/shard_map/chebyshev/pallas_call | solution.py:475
  48.3 0.7 %copy.11 = f32[512,128]{1,0:T(8,128)} copy(f32[512,128]{1,0:T(8,128)S(1)} %get-tuple-element.6) | data formatting | bytes 524288

commit v6 on v5

--- a/solution.py
+++ b/solution.py
@@ -461,7 +461,7 @@
             terms = [sum(terms[i:i + 2][1:], terms[i]) for i in range(0, len(terms), 2)]
         mine = terms[0]
         base += size
-    norm_ref[0, 0] = jnp.sqrt(jnp.sum(mine, axis=1, keepdims=True))[0, 0]
+    norm_ref[...] = jnp.sqrt(jnp.sum(mine, axis=1, keepdims=True))
 
 
 def solution(mesh):
@@ -471,15 +471,14 @@
     def local(wavefunctions, cell_matrix, cell_nodes, home_counts, atom_start, projectors, coupling):
         hbm = pl.BlockSpec(memory_space=pl.ANY)
         vmem = pl.BlockSpec(memory_space=pltpu.VMEM)
-        smem = pl.BlockSpec(memory_space=pltpu.SMEM)
         filtered, norm = pl.pallas_call(
             functools.partial(kernel, ny),
             out_shape=(
                 pltpu.VMEM((OWN, COLS), F32),
-                jax.ShapeDtypeStruct((1, 1), F32),
+                pltpu.VMEM((1, 1), F32),
             ),
             in_specs=[hbm] * 7,
-            out_specs=(vmem, smem),
+            out_specs=(vmem, vmem),
             scratch_shapes=[
                 pltpu.VMEM((4, OWN, COLS), F32),
                 pltpu.VMEM((3, OWN, COLS), BF16),

time: 50.9 us -> 49.8 us (0.978)
  Pallas kernels: 47.7 us -> 47.1 us
  between operations: 2.33 us -> 1.8 us
    pallas_call x1, Pallas kernels: 47.7 us -> 47.1 us  [local(): pl.pallas_call(functools.partial(kernel, ny), out_shape=(pltpu.VMEM((OWN,...]
where the time goes in v6:
time: 49.8 us; the launch traced here: 49.6 us
  Pallas kernels  47.1 us (95%)
  between operations  1.8 us (4%)
  local copies, waits for them, and re-layouts  0.71 us (1%)
    pallas_call x1, Pallas kernels, local(): pl.pallas_call(functools.partial(kernel, ny), out_shape=(pltpu.VMEM((OWN,...  47.1 us

profile of v6, /device:TPU:1, one launch (start us, length us, event | category | flops | bytes accessed | tf_op | source)
XLA Modules:
  0.0 49.6 jit_solution(9801467942772702858)
XLA Ops:
  0.6 47.1 %chebyshev.1 = (f32[512,128]{1,0:T(8,128)S(1)}, f32[1,1]{1,0:T(1,128)S(1)}) custom-call(f32[512,128]{1,0:T(8,128)} %wave_ref.1, bf16[2,512,512]{2,1,0:T(8,128)(2,1)} %matrix_ref.1, s32[2,512]{1,0:T(2,128)} %nodes_hbm.1, s32[1,3]{1,0:T(1,128)} %counts_hbm.1, s32[3,1,4]{2,1,0:T(1,128)} %bitcast.6, bf16[1,3,18,4,256]{4,3,2,1,0:T(4,128)(2,1)} %bitcast.4, ...), custom_call_target="tpu_custom_call" | custom-call | tf_op jit(solution)/shard_map/chebyshev/pallas_call | solution.py:474
  47.8 0.7 %copy.11 = f32[512,128]{1,0:T(8,128)} copy(f32[512,128]{1,0:T(8,128)S(1)} %get-tuple-element.6) | data formatting | bytes 524288
